TPU v7x, 32 devices: a whole 2x2x4 slice. The times are simulated.
32 devices in a mesh: phase: 4 (over y, x), slab: 8 (over z, core).
Axes of the slice: x: 2, y: 2, z: 4, core: 2. Of those that a mesh axis runs over, the one named last changes fastest.
Arguments:
- images: float32 [8, 256, 64, 128], P('phase', 'slab'), may hold values from -8 to 8, as said below
Outputs:
- forces: float32 [3, 8, 256, 64, 128], P(None, 'phase', 'slab')
Inputs may be any that keep to these rules, and one draw needn't show every extreme that they name: `images`: Breathing-phase volumes of one body.
All inputs are finite; a program needn't handle non-finite values.
Results may differ from a plain program's by a relative error of at most 0.0001.
Values sent between devices are 32-bit elements; how exact they have to be, the bound alone decides.
No kernel may reach another device: no remote copies, remote signals or barrier semaphores. Data moves between devices by JAX's collectives and lax.ppermute only.
A program may use at most 128 MiB of HBM per device.

v0:
```python
import functools

import jax
import jax.numpy as jnp
from jax import lax
from jax.experimental import pallas as pl
from jax.experimental.pallas import tpu as pltpu
from jax.sharding import PartitionSpec as P


EPSILON = 1e-05
CELLS = 729.0
BLOCK = 4
VMEM = pl.BlockSpec(memory_space=pltpu.VMEM)
ANY = pl.BlockSpec(memory_space=pl.ANY)
GRANT = 10


def box_matrix(width):
    i = lax.broadcasted_iota(jnp.int32, (width, width), 0)
    j = lax.broadcasted_iota(jnp.int32, (width, width), 1)
    band = jnp.where(jnp.abs(i - j) <= 4, 1.0, 0.0).astype(jnp.bfloat16)
    return jnp.concatenate([band, band, band], axis=0)


def thirds(v):
    high = v.astype(jnp.bfloat16)
    rest = v - high.astype(jnp.float32)
    middle = rest.astype(jnp.bfloat16)
    low = (rest - middle.astype(jnp.float32)).astype(jnp.bfloat16)
    return jnp.concatenate([high, middle, low], axis=1)


def depth_sums(p):
    core = ((p[3] + p[4]) + (p[5] + p[6])) + (p[7] + p[8])
    a = p[1] + p[2]
    b = p[9] + p[10]
    return (core + (p[0] + a), core + (a + p[9]), core + (p[2] + b), core + (b + p[11]))


def clear_rims(tz, rows):
    zero = jnp.zeros((8, tz.shape[-1]), jnp.float32)
    for w in range(tz.shape[0]):
        for i in range(BLOCK):
            tz[w, i, 0:8, :] = zero
            tz[w, i, rows + 8 : rows + 16, :] = zero


def plane_sums(i, tz, t3, sx, box):
    windows, rows = tz.shape[0], tz.shape[2] - 16
    parts = []
    for w in range(windows):
        for k in range(rows // 8 + 1):
            r = 8 * k
            t3[i, w, r : r + 8, :] = (
                tz[w, i, r + 3 : r + 11, :] + tz[w, i, r + 4 : r + 12, :] + tz[w, i, r + 5 : r + 13, :]
            )
        parts.append(
            thirds(t3[i, w, 1 : rows + 1, :] + t3[i, w, 4 : rows + 4, :] + t3[i, w, 7 : rows + 7, :])
        )
    sums = jnp.dot(jnp.concatenate(parts, axis=0), box, preferred_element_type=jnp.float32)
    for w in range(windows):
        sx[w, i] = sums[rows * w : rows * (w + 1)]


def pair_weight(s_both, s_a, s_b, v_a, v_b):
    c = CELLS * s_both - s_a * s_b
    return c, c * (2.0 * CELLS * CELLS) / (v_a * v_b + EPSILON * CELLS**4)


def plane_of(parts, base):
    def read(a, p, rows):
        z = base + p
        for ref, offset, first, length in parts:
            if first <= z < first + length:
                return ref[a + offset, z - first, rows, :]
        raise ValueError("plane")

    return read


def own_block(read, stats, acc, z_out, tz, t3, sx, box):
    rows = tz.shape[2] - 16

    @pl.loop(0, rows // 8)
    def _(y):
        here = pl.ds(pl.multiple_of(y * 8, 8), 8)
        there = pl.ds(pl.multiple_of(y * 8 + 8, 8), 8)

        def put(w, planes):
            for i, v in enumerate(depth_sums(planes)):
                tz[w, i, there, :] = v

        zero = [read(0, p, here) for p in range(12)]
        put(0, zero)
        put(1, [v * v for v in zero])
        one = [read(1, p, here) for p in range(12)]
        put(2, one)
        put(3, [v * v for v in one])
        put(4, [v * read(0, p, here) for p, v in enumerate(one)])

    for i in range(BLOCK):
        plane_sums(i, tz, t3, sx, box)
        for y in range(0, rows, 8):
            r = slice(y, y + 8)
            s_0, q_0, s_1, q_1, both = [sx[w, i, r, :] for w in range(5)]
            v_0 = CELLS * q_0 - s_0 * s_0
            v_1 = CELLS * q_1 - s_1 * s_1
            c, g = pair_weight(both, s_0, s_1, v_0, v_1)
            z = z_out + i
            stats[0, 0, z, r, :] = s_0
            stats[0, 1, z, r, :] = v_0
            stats[1, 0, z, r, :] = s_1
            stats[1, 1, z, r, :] = v_1
            acc[0, 0, z, r, :] = g * (read(1, BLOCK + i, r) - s_1 * (1.0 / CELLS))
            acc[1, 0, z, r, :] = g * (read(0, BLOCK + i, r) - s_0 * (1.0 / CELLS))
            gc = g * c
            acc[0, 1, z, r, :] = gc
            acc[1, 1, z, r, :] = gc


def own_inner_kernel(size, *refs):
    parts, (stats, acc, field, tz, t3, sx) = refs[: size + 2], refs[size + 2 :]
    rows, width = parts[0].shape[2:]
    clear_rims(tz, rows)
    box = box_matrix(width)
    for k, part in enumerate(parts):
        for a in range(2):
            field[a, BLOCK * k : BLOCK * (k + 1)] = part[a]

    @pl.loop(0, size)
    def _(j):
        own_block(lambda a, p, rows: field[a, BLOCK * j + p, rows, :], stats, acc, BLOCK * j, tz, t3, sx, box)


def own_ends_kernel(low, high, first, second, third, fourth, stats, acc, field, tz, t3, sx):
    rows, width = first.shape[2:]
    clear_rims(tz, rows)
    box = box_matrix(width)
    for e, parts in enumerate(((low, first, second), (third, fourth, high))):
        for k, part in enumerate(parts):
            for a in range(2):
                field[e, a, BLOCK * k : BLOCK * (k + 1)] = part[a]

    @pl.loop(0, 2)
    def _(e):
        own_block(lambda a, p, rows: field[e, a, p, rows, :], stats, acc, BLOCK * e, tz, t3, sx, box)


def side_block(near, own, theirs, centre, stats, stats_base, acc, acc_base, tz, t3, sx, box, sink):
    rows = tz.shape[2] - 16
    far = 1 - near
    own_near, own_far = far, near

    @pl.loop(0, rows // 8)
    def _(y):
        here = pl.ds(pl.multiple_of(y * 8, 8), 8)
        there = pl.ds(pl.multiple_of(y * 8 + 8, 8), 8)

        def put(w, planes):
            for i, v in enumerate(depth_sums(planes)):
                tz[w, i, there, :] = v

        n = [theirs(near, p, here) for p in range(12)]
        put(0, n)
        put(1, [v * v for v in n])
        put(2, [v * own(own_near, p, here) for p, v in enumerate(n)])
        put(3, [v * own(own_far, p, here) for p, v in enumerate(n)])
        f = [theirs(far, p, here) for p in range(12)]
        put(4, f)
        put(5, [v * v for v in f])
        put(6, [v * own(own_near, p, here) for p, v in enumerate(f)])

    for i in range(BLOCK):
        plane_sums(i, tz, t3, sx, box)
        z = stats_base + i
        b = acc_base + i
        for y in range(0, rows, 8):
            r = slice(y, y + 8)
            s_n, q_n, nn, fn, s_f, q_f, nf = [sx[w, i, r, :] for w in range(7)]
            o_s, o_v = stats[own_near, 0, z, r, :], stats[own_near, 1, z, r, :]
            p_s, p_v = stats[own_far, 0, z, r, :], stats[own_far, 1, z, r, :]
            v_n = CELLS * q_n - s_n * s_n
            v_f = CELLS * q_f - s_f * s_f
            off_n = centre[near, i, r, :] - s_n * (1.0 / CELLS)
            off_f = centre[far, i, r, :] - s_f * (1.0 / CELLS)
            c_nn, g_nn = pair_weight(nn, o_s, s_n, o_v, v_n)
            c_nf, g_nf = pair_weight(nf, o_s, s_f, o_v, v_f)
            c_fn, g_fn = pair_weight(fn, p_s, s_n, p_v, v_n)
            sink(own_near, i, r, acc[own_near, 0, b, r, :] + g_nn * off_n + g_nf * off_f,
                 acc[own_near, 1, b, r, :] + g_nn * c_nn + g_nf * c_nf, o_s, o_v)
            sink(own_far, i, r, acc[own_far, 0, b, r, :] + g_fn * off_n,
                 acc[own_far, 1, b, r, :] + g_fn * c_fn, p_s, p_v)


def readers(j, count, side, refs):
    depth = BLOCK * count
    own = [(ref, 0, BLOCK * k[1], BLOCK) for k, ref in refs.items() if k[0] == "own"]
    theirs = [(ref, 0, BLOCK * k[1], BLOCK) for k, ref in refs.items() if k[0] == "side"]
    for name, first in (("low", -BLOCK), ("high", depth)):
        if (name,) in refs:
            own.append((refs[name,], 0, first, BLOCK))
            theirs.append((refs[name,], 2 * side, first, BLOCK))
    base = BLOCK * (j - 1)
    return plane_of(own, base), plane_of(theirs, base)


def split_refs(keys, refs):
    return dict(zip(keys, refs[: len(keys)])), refs[len(keys) :]


def first_kernel(j, count, stats_base, keys, *refs):
    refs, (out, tz, t3, sx) = split_refs(keys, refs)
    near = lax.rem(lax.axis_index("phase"), 2)
    rows, width = refs["own", j].shape[2:]
    clear_rims(tz, rows)
    own, theirs = readers(j, count, 1, refs)

    def sink(a, i, r, one, two, s, v):
        out[a, 0, i, r, :] = one
        out[a, 1, i, r, :] = two

    side_block(near, own, theirs, refs["side", j], refs["stats", j], stats_base, refs["acc", j], stats_base,
               tz, t3, sx, box_matrix(width), sink)


def last_kernel(js, count, bases, keys, *refs):
    refs, (out, tz, t3, sx, coef, padded, block, sems) = split_refs(keys, refs)
    near = 1 - lax.rem(lax.axis_index("phase"), 2)
    rows, width = refs["own", js[0]].shape[2:]
    clear_rims(tz, rows)
    zero = jnp.zeros((8, width), jnp.float32)
    for a in range(2):
        padded[a, 0:8, :] = zero
        padded[a, rows + 8 : rows + 16, :] = zero
    lane = lax.broadcasted_iota(jnp.int32, (8, width), 1)
    box = box_matrix(width)
    copies = []
    for n, j in enumerate(js):
        own, theirs = readers(j, count, 2, refs)

        def sink(a, i, r, one, two, s, v):
            here = own(a, BLOCK + i, r)
            coef[a, i, r, :] = 0.5 * (
                one - two / (v + EPSILON * CELLS * CELLS) * (here - s * (1.0 / CELLS))
            )

        side_block(near, own, theirs, refs["side", j], refs["stats", j], bases[n], refs["acc", j], 0,
                   tz, t3, sx, box, sink)
        for i in range(BLOCK):
            for a in range(2):
                padded[a, 8 : rows + 8, :] = refs["own", j][a, i]
                for y in range(0, rows, 8):
                    r = slice(y, y + 8)
                    c = coef[a, i, r, :]
                    block[n, 0, a, i, r, :] = c * (own(a, i + 5, r) - own(a, i + 3, r))
                    block[n, 1, a, i, r, :] = c * (padded[a, y + 9 : y + 17, :] - padded[a, y + 7 : y + 15, :])
                    v = padded[a, y + 8 : y + 16, :]
                    after_x = jnp.where(lane < width - 1, pltpu.roll(v, width - 1, 1), 0.0)
                    before_x = jnp.where(lane > 0, pltpu.roll(v, 1, 1), 0.0)
                    block[n, 2, a, i, r, :] = c * (after_x - before_x)
        copy = pltpu.make_async_copy(block.at[n], out.at[:, :, BLOCK * j : BLOCK * (j + 1)], sems.at[n])
        copy.start()
        copies.append(copy)
    for copy in copies:
        copy.wait()


def scratches(windows, rows, width):
    return [
        pltpu.VMEM((windows, BLOCK, rows + 16, width), jnp.float32),
        pltpu.VMEM((BLOCK, windows, rows + 8, width), jnp.float32),
        pltpu.VMEM((windows, BLOCK, rows, width), jnp.float32),
    ]


def params(mib=GRANT):
    return pltpu.CompilerParams(vmem_limit_bytes=mib << 20)


def like(*shape):
    return jax.ShapeDtypeStruct(shape, jnp.float32)


def cut_kernel(bs, images, *refs):
    outs, sems = refs[:-1], refs[-1]
    copies = [
        pltpu.make_async_copy(images.at[:, BLOCK * b : BLOCK * (b + 1)], outs[n], sems.at[n]) for n, b in enumerate(bs)
    ]
    for copy in copies:
        copy.start()
    for copy in copies:
        copy.wait()


def cut_blocks(bs, images, mib):
    phases, _, rows, width = images.shape
    outs = pl.pallas_call(
        functools.partial(cut_kernel, bs),
        out_shape=[like(phases, BLOCK, rows, width)] * len(bs),
        in_specs=[pl.BlockSpec(memory_space=pltpu.HBM)],
        out_specs=[VMEM] * len(bs),
        scratch_shapes=[pltpu.SemaphoreType.DMA((len(bs),))],
        compiler_params=params(mib),
    )(pltpu.with_memory_space_constraint(images, pltpu.HBM))
    return dict(zip(bs, outs))


def pack_kernel(*refs):
    for n in range(2):
        for k in range(3):
            for a in range(2):
                refs[6 + n][2 * k + a] = refs[3 * n + k][a]


def packed(groups):
    shape = groups[0][0].shape
    out = like(3 * shape[0], *shape[1:])
    return pl.pallas_call(
        pack_kernel,
        out_shape=(out, out),
        in_specs=[VMEM] * 6,
        out_specs=(VMEM, VMEM),
        compiler_params=params(6),
        name="pack",
    )(*groups[0], *groups[1])


def own_inner(low, high, blocks):
    rows, width = blocks[low].shape[2:]
    size = high - low
    shape = like(2, 2, BLOCK * size, rows, width)
    return pl.pallas_call(
        functools.partial(own_inner_kernel, size),
        out_shape=(shape, shape),
        in_specs=[VMEM] * (size + 2),
        out_specs=(VMEM, VMEM),
        scratch_shapes=[pltpu.VMEM((2, BLOCK * (size + 2), rows, width), jnp.float32)] + scratches(5, rows, width),
        compiler_params=params(),
    )(*[blocks[b] for b in range(low - 1, high + 1)])


def own_ends(low, high, *blocks):
    rows, width = low.shape[2:]
    shape = like(2, 2, 2 * BLOCK, rows, width)
    return pl.pallas_call(
        own_ends_kernel,
        out_shape=(shape, shape),
        in_specs=[VMEM] * 6,
        out_specs=(VMEM, VMEM),
        scratch_shapes=[pltpu.VMEM((2, 2, 3 * BLOCK, rows, width), jnp.float32)] + scratches(5, rows, width),
        compiler_params=params(),
        name="own_ends",
    )(low, high, *blocks)


def gather_operands(js, count, own, side, low, high):
    wanted = {}
    for j in js:
        for b in (j - 1, j, j + 1):
            if b < 0:
                wanted["low",] = low
            elif b >= count:
                wanted["high",] = high
            else:
                wanted["own", b] = own[b]
                wanted["side", b] = side[b]
    return wanted


def specs_of(wanted):
    return [ANY if k == ("forces",) else VMEM for k in wanted]


def first_side(j, count, own, side, low, high, stats, acc, base):
    rows, width = low.shape[2:]
    wanted = gather_operands((j,), count, own, side, low, high)
    wanted["stats", j], wanted["acc", j] = stats, acc
    return pl.pallas_call(
        functools.partial(first_kernel, j, count, base, tuple(wanted)),
        out_shape=like(2, 2, BLOCK, rows, width),
        in_specs=specs_of(wanted),
        out_specs=VMEM,
        scratch_shapes=scratches(7, rows, width),
        compiler_params=params(),
    )(*wanted.values())


def last_side(js, count, own, side, low, high, stats, bases, accs, forces):
    rows, width = low.shape[2:]
    depth = BLOCK * count
    wanted = gather_operands(js, count, own, side, low, high)
    for j in js:
        wanted["stats", j] = stats[j]
        wanted["acc", j] = accs[j]
    if forces is not None:
        wanted["forces",] = forces
    return pl.pallas_call(
        functools.partial(last_kernel, js, count, [bases[j] for j in js], tuple(wanted)),
        out_shape=like(3, 2, depth, rows, width),
        in_specs=specs_of(wanted),
        out_specs=ANY,
        input_output_aliases={len(wanted) - 1: 0} if forces is not None else {},
        scratch_shapes=scratches(7, rows, width)
        + [
            pltpu.VMEM((2, BLOCK, rows, width), jnp.float32),
            pltpu.VMEM((2, rows + 16, width), jnp.float32),
            pltpu.VMEM((len(js), 3, 2, BLOCK, rows, width), jnp.float32),
            pltpu.SemaphoreType.DMA((len(js),)),
        ],
        compiler_params=params(),
    )(*wanted.values())


def across(value):
    n = lax.axis_size("phase")
    return lax.ppermute(value, "phase", [(q, q ^ 1) for q in range(n)])


def onward(value):
    n = lax.axis_size("phase")
    return lax.ppermute(value, "phase", [(q, (q + (2 if q % 2 == 0 else n - 2)) % n) for q in range(n)])


def upward(value):
    n = lax.axis_size("slab")
    return lax.ppermute(value, "slab", [(q, q + 1) for q in range(n - 1)])


def downward(value):
    n = lax.axis_size("slab")
    return lax.ppermute(value, "slab", [(q + 1, q) for q in range(n - 1)])


def local_forces(images):
    count = images.shape[1] // BLOCK
    assert images.shape[0] == 2 and images.shape[1] == BLOCK * count and count >= 6
    assert lax.axis_size("phase") % 2 == 0
    half = (count + 1) // 2

    blocks = cut_blocks((0, count - 1), images, 4)
    blocks.update(cut_blocks(tuple(range(1, count - 1)), images, 4))
    one = {b: across(blocks[b]) for b in blocks}
    two = {b: onward(one[b]) for b in blocks}
    top, end = 0, count - 1
    low, high = packed([(blocks[end], one[end], two[end]), (blocks[top], one[top], two[top])])
    low, high = upward(low), downward(high)

    near_half = own_inner(1, half, blocks)
    far_half = own_inner(half, count - 1, blocks)
    outer = own_ends(low, high, blocks[0], blocks[1], blocks[end - 1], blocks[end])
    stats, acc, base = {}, {}, {}
    for j in range(count):
        if j in (0, count - 1):
            (stats[j], acc[j]), base[j] = outer, 0 if j == 0 else BLOCK
        elif j < half:
            (stats[j], acc[j]), base[j] = near_half, BLOCK * (j - 1)
        else:
            (stats[j], acc[j]), base[j] = far_half, BLOCK * (j - half)
    sums = {
        j: first_side(j, count, blocks, one, low, high, stats[j], acc[j], base[j]) for j in range(count)
    }
    forces = None
    for js in last_groups(count):
        forces = last_side(js, count, blocks, two, low, high, stats, base, sums, forces)
    return forces


def last_groups(count):
    return [(j,) for j in [1, 2, 0] + list(range(3, count - 3))] + [tuple(range(count - 3, count))]


def solution(mesh):
    in_specs = (P("phase", "slab", None, None),)
    out_specs = P(None, "phase", "slab", None, None)
    return jax.shard_map(local_forces, mesh=mesh, in_specs=in_specs, out_specs=out_specs, check_vma=False)
```

profile of v0, /device:TPU:16, one launch (start us, length us, event | category | flops | bytes accessed | tf_op | source)
XLA Modules:
  0.0 94.9 jit_solution(8745897958360486135)
XLA Ops:
  1.1 1.6 %collective-permute-start.8 = (f32[2,4,64,128]{3,2,1,0:T(8,128)S(1)}, f32[2,4,64,128]{3,2,1,0:T(8,128)S(1)}, u32[]{:S(2)}, u32[]{:S(2)}) collective-permute-start(f32[2,4,64,128]{3,2,1,0:T(8,128)S(1)} %get-tuple-element.25.refs_3_.first.refs_0_.refs_1_), channel_id=1, source_target_pairs={{0,8},{8,0},{16,24},{24,16},{1,9},{9,1},{17,25},{25,17},{2,10},{10... | collective-permute-start | bytes 786440 | tf_op jit(solution)/shard_map/ppermute | solution.py:417
  3.1 7.1 %collective-permute-done.8.refs_4_.refs_2_.refs_1_ = f32[2,4,64,128]{3,2,1,0:T(8,128)S(1)} collective-permute-done((f32[2,4,64,128]{3,2,1,0:T(8,128)S(1)}, f32[2,4,64,128]{3,2,1,0:T(8,128)S(1)}, u32[]{:S(2)}, u32[]{:S(2)}) %collective-permute-start.8) | collective-permute-done | bytes 262176 | tf_op jit(solution)/shard_map/ppermute | solution.py:417
  10.3 1.5 %collective-permute-start.9 = (f32[2,4,64,128]{3,2,1,0:T(8,128)S(1)}, f32[2,4,64,128]{3,2,1,0:T(8,128)S(1)}, u32[]{:S(2)}, u32[]{:S(2)}) collective-permute-start(f32[2,4,64,128]{3,2,1,0:T(8,128)S(1)} %collective-permute-done.8.refs_4_.refs_2_.refs_1_), channel_id=1, source_target_pairs={{0,16},{8,24},{16,0},{24,8},{1,17},{9,25},{17,1},{25,9},{2,18},{10... | collective-permute-start | bytes 786440 | tf_op jit(solution)/shard_map/ppermute | solution.py:422
  11.8 3.0 %collective-permute-done.6.refs_1_.refs_5_.refs_3_ = f32[2,4,64,128]{3,2,1,0:T(8,128)S(1)} collective-permute-done((f32[2,4,64,128]{3,2,1,0:T(8,128)S(1)}, f32[2,4,64,128]{3,2,1,0:T(8,128)S(1)}, u32[]{:S(2)}, u32[]{:S(2)}) %collective-permute-start.6) | collective-permute-done | bytes 262176 | tf_op jit(solution)/shard_map/ppermute | solution.py:417
  17.7 1.6 %collective-permute-start.16 = (f32[2,4,64,128]{3,2,1,0:T(8,128)S(1)}, f32[2,4,64,128]{3,2,1,0:T(8,128)S(1)}, u32[]{:S(2)}, u32[]{:S(2)}) collective-permute-start(f32[2,4,64,128]{3,2,1,0:T(8,128)S(1)} %get-tuple-element.31.second.refs_1_.refs_3_.refs_0_.refs_2_), channel_id=1, source_target_pairs={{0,8},{8,0},{16,24},{24,16},{1,9},{9,1},{17,25},{25,17},{2,10},{10... | collective-permute-start | bytes 786440 | tf_op jit(solution)/shard_map/ppermute | solution.py:417
  22.4 1.9 %collective-permute-start.10 = (f32[6,4,64,128]{3,2,1,0:T(8,128)S(1)}, f32[6,4,64,128]{3,2,1,0:T(8,128)S(1)}, u32[]{:S(2)}, u32[]{:S(2)}) collective-permute-start(f32[6,4,64,128]{3,2,1,0:T(8,128)S(1)} %get-tuple-element.26), channel_id=1, source_target_pairs={{1,0},{2,1},{3,2},{4,3},{5,4},{6,5},{7,6},{9,8},{10,9},{11,10},{12... | collective-permute-start | bytes 2359304 | tf_op jit(solution)/shard_map/ppermute | solution.py:432
  24.3 2.4 %collective-permute-start.11 = (f32[6,4,64,128]{3,2,1,0:T(8,128)S(1)}, f32[6,4,64,128]{3,2,1,0:T(8,128)S(1)}, u32[]{:S(2)}, u32[]{:S(2)}) collective-permute-start(f32[6,4,64,128]{3,2,1,0:T(8,128)S(1)} %get-tuple-element.30), channel_id=1, source_target_pairs={{0,1},{1,2},{2,3},{3,4},{4,5},{5,6},{6,7},{8,9},{9,10},{10,11},{11... | collective-permute-start | bytes 2359304 | tf_op jit(solution)/shard_map/ppermute | solution.py:427
  28.4 4.1 %collective-permute-done.14.refs_1_.refs_3_.refs_5_ = f32[2,4,64,128]{3,2,1,0:T(8,128)S(1)} collective-permute-done((f32[2,4,64,128]{3,2,1,0:T(8,128)S(1)}, f32[2,4,64,128]{3,2,1,0:T(8,128)S(1)}, u32[]{:S(2)}, u32[]{:S(2)}) %collective-permute-start.14) | collective-permute-done | bytes 262176 | tf_op jit(solution)/shard_map/ppermute | solution.py:417
  34.1 4.1 %collective-permute-done.12.refs_1_.refs_3_.refs_5_ = f32[2,4,64,128]{3,2,1,0:T(8,128)S(1)} collective-permute-done((f32[2,4,64,128]{3,2,1,0:T(8,128)S(1)}, f32[2,4,64,128]{3,2,1,0:T(8,128)S(1)}, u32[]{:S(2)}, u32[]{:S(2)}) %collective-permute-start.12) | collective-permute-done | bytes 262176 | tf_op jit(solution)/shard_map/ppermute | solution.py:417
  39.7 4.1 %collective-permute-done.refs_1_.refs_3_.refs_5_ = f32[2,4,64,128]{3,2,1,0:T(8,128)S(1)} collective-permute-done((f32[2,4,64,128]{3,2,1,0:T(8,128)S(1)}, f32[2,4,64,128]{3,2,1,0:T(8,128)S(1)}, u32[]{:S(2)}, u32[]{:S(2)}) %collective-permute-start) | collective-permute-done | bytes 262176 | tf_op jit(solution)/shard_map/ppermute | solution.py:417
  44.3 5.1 %collective-permute-done.2.refs_3_.refs_1_.refs_5_ = f32[2,4,64,128]{3,2,1,0:T(8,128)S(1)} collective-permute-done((f32[2,4,64,128]{3,2,1,0:T(8,128)S(1)}, f32[2,4,64,128]{3,2,1,0:T(8,128)S(1)}, u32[]{:S(2)}, u32[]{:S(2)}) %collective-permute-start.2) | collective-permute-done | bytes 262176 | tf_op jit(solution)/shard_map/ppermute | solution.py:417
  49.9 2.8 %collective-permute-done.4.refs_5_.refs_3_.refs_1_ = f32[2,4,64,128]{3,2,1,0:T(8,128)S(1)} collective-permute-done((f32[2,4,64,128]{3,2,1,0:T(8,128)S(1)}, f32[2,4,64,128]{3,2,1,0:T(8,128)S(1)}, u32[]{:S(2)}, u32[]{:S(2)}) %collective-permute-start.4) | collective-permute-done | bytes 262176 | tf_op jit(solution)/shard_map/ppermute | solution.py:417
  53.3 1.5 %collective-permute-start.1 = (f32[2,4,64,128]{3,2,1,0:T(8,128)S(1)}, f32[2,4,64,128]{3,2,1,0:T(8,128)S(1)}, u32[]{:S(2)}, u32[]{:S(2)}) collective-permute-start(f32[2,4,64,128]{3,2,1,0:T(8,128)S(1)} %collective-permute-done.refs_1_.refs_3_.refs_5_), channel_id=1, source_target_pairs={{0,16},{8,24},{16,0},{24,8},{1,17},{9,25},{17,1},{25,9},{2,18},{10... | collective-permute-start | bytes 786440 | tf_op jit(solution)/shard_map/ppermute | solution.py:422
  54.8 3.6 %collective-permute-done.15.refs_5_.refs_3_.refs_1_ = f32[2,4,64,128]{3,2,1,0:T(8,128)S(1)} collective-permute-done((f32[2,4,64,128]{3,2,1,0:T(8,128)S(1)}, f32[2,4,64,128]{3,2,1,0:T(8,128)S(1)}, u32[]{:S(2)}, u32[]{:S(2)}) %collective-permute-start.15) | collective-permute-done | bytes 262176 | tf_op jit(solution)/shard_map/ppermute | solution.py:422
  58.9 5.1 %collective-permute-done.13.refs_5_.refs_3_.refs_1_ = f32[2,4,64,128]{3,2,1,0:T(8,128)S(1)} collective-permute-done((f32[2,4,64,128]{3,2,1,0:T(8,128)S(1)}, f32[2,4,64,128]{3,2,1,0:T(8,128)S(1)}, u32[]{:S(2)}, u32[]{:S(2)}) %collective-permute-start.13) | collective-permute-done | bytes 262176 | tf_op jit(solution)/shard_map/ppermute | solution.py:422
  64.5 2.2 %shard_map.24 = (f32[2,2,12,64,128]{4,3,2,1,0:T(8,128)S(1)}, f32[2,2,12,64,128]{4,3,2,1,0:T(8,128)S(1)}) custom-call(f32[2,4,64,128]{3,2,1,0:T(8,128)S(1)} %get-tuple-element.25.refs_3_.first.refs_0_.refs_1_, f32[2,4,64,128]{3,2,1,0:T(8,128)S(1)} %get-tuple-element.31.second.refs_1_.refs_3_.refs_0_.refs_2_, ...), custom_call_target="tpu_custom_call" | custom-call | tf_op jit(solution)/shard_map/pallas_call | solution.py:333
  66.7 2.2 %shard_map.19 = (f32[2,2,12,64,128]{4,3,2,1,0:T(8,128)S(1)}, f32[2,2,12,64,128]{4,3,2,1,0:T(8,128)S(1)}) custom-call(f32[2,4,64,128]{3,2,1,0:T(8,128)S(1)} %get-tuple-element.27.refs_0_.refs_3_.refs_2_.refs_4_, f32[2,4,64,128]{3,2,1,0:T(8,128)S(1)} %get-tuple-element.21.refs_1_.refs_0_.refs_2_.refs_4_, ...), custom_call_target="tpu_custom_call" | custom-call | tf_op jit(solution)/shard_map/pallas_call | solution.py:333
  75.4 2.2 %shard_map.29.refs_8_ = f32[3,2,32,64,128]{4,3,2,1,0:T(8,128)} custom-call(f32[2,4,64,128]{3,2,1,0:T(8,128)S(1)} %get-tuple-element.25.refs_3_.first.refs_0_.refs_1_, f32[2,4,64,128]{3,2,1,0:T(8,128)S(1)} %collective-permute-done.9.refs_5_.refs_1_.refs_2_, f32[2,4,64,128]{3,2,1,0:T(8,128)S(1)} %get-tuple-element.31.second.refs_1_.refs_3_.refs_0_.refs_2_, ...), custom_call_target="tpu_custom_call" | custom-call | tf_op jit(solution)/shard_map/pallas_call | solution.py:398
  77.6 2.2 %shard_map.30.refs_7_ = f32[3,2,32,64,128]{4,3,2,1,0:T(8,128)} custom-call(f32[2,4,64,128]{3,2,1,0:T(8,128)S(1)} %get-tuple-element.31.second.refs_1_.refs_3_.refs_0_.refs_2_, f32[2,4,64,128]{3,2,1,0:T(8,128)S(1)} %collective-permute-done.17.refs_3_.refs_1_.refs_4_, ...), custom_call_target="tpu_custom_call", output_to_operand_aliasing={{}: (8, {})} | custom-call | tf_op jit(solution)/shard_map/pallas_call | solution.py:398
  79.8 1.5 %own_ends.1 = (f32[2,2,8,64,128]{4,3,2,1,0:T(8,128)S(1)}, f32[2,2,8,64,128]{4,3,2,1,0:T(8,128)S(1)}) custom-call(f32[6,4,64,128]{3,2,1,0:T(8,128)S(1)} %collective-permute-done.11.low.refs_0_, f32[6,4,64,128]{3,2,1,0:T(8,128)S(1)} %collective-permute-done.10.high.refs_4_.refs_8_, f32[2,4,64,128]{3,2,1,0:T(8,128)S(1)} %get-tuple-element.25.refs_3_.first.refs_0_.refs_1_, ...), custom_call_target="tpu_custom_call" | custom-call | tf_op jit(solution)/shard_map/own_ends/pallas_call | solution.py:346
  83.4 2.2 %shard_map.31.refs_8_ = f32[3,2,32,64,128]{4,3,2,1,0:T(8,128)} custom-call(f32[6,4,64,128]{3,2,1,0:T(8,128)S(1)} %collective-permute-done.11.low.refs_0_, f32[2,4,64,128]{3,2,1,0:T(8,128)S(1)} %get-tuple-element.25.refs_3_.first.refs_0_.refs_1_, f32[2,4,64,128]{3,2,1,0:T(8,128)S(1)} %collective-permute-done.9.refs_5_.refs_1_.refs_2_, ...), custom_call_target="tpu_custom_call", output_to_operand_aliasing={{}: (7, {})} | custom-call | tf_op jit(solution)/shard_map/pallas_call | solution.py:398
  85.6 2.2 %shard_map.32.refs_8_ = f32[3,2,32,64,128]{4,3,2,1,0:T(8,128)} custom-call(f32[2,4,64,128]{3,2,1,0:T(8,128)S(1)} %get-tuple-element.34.refs_2_.refs_0_.refs_4_, f32[2,4,64,128]{3,2,1,0:T(8,128)S(1)} %collective-permute-done.15.refs_5_.refs_3_.refs_1_, ...), custom_call_target="tpu_custom_call", output_to_operand_aliasing={{}: (8, {})} | custom-call | tf_op jit(solution)/shard_map/pallas_call | solution.py:398
  87.8 2.3 %shard_map.33.refs_15_ = f32[3,2,32,64,128]{4,3,2,1,0:T(8,128)} custom-call(f32[2,4,64,128]{3,2,1,0:T(8,128)S(1)} %get-tuple-element.27.refs_0_.refs_3_.refs_2_.refs_4_, f32[2,4,64,128]{3,2,1,0:T(8,128)S(1)} %collective-permute-done.13.refs_5_.refs_3_.refs_1_, ...), custom_call_target="tpu_custom_call", output_to_operand_aliasing={{}: (8, {})} | custom-call | tf_op jit(solution)/shard_map/pallas_call | solution.py:398
  90.1 4.5 %shard_map.34 = f32[3,2,32,64,128]{4,3,2,1,0:T(8,128)} custom-call(f32[2,4,64,128]{3,2,1,0:T(8,128)S(1)} %get-tuple-element.21.refs_1_.refs_0_.refs_2_.refs_4_, f32[2,4,64,128]{3,2,1,0:T(8,128)S(1)} %collective-permute-done.1.refs_5_.refs_3_.refs_1_, ...), custom_call_target="tpu_custom_call", output_to_operand_aliasing={{}: (15, {})} | custom-call | tf_op jit(solution)/shard_map/pallas_call | solution.py:398
  (32 shorter events, 23.4 us)
Async XLA Ops:
  1.1 9.2 %collective-permute-start.8 = (f32[2,4,64,128]{3,2,1,0:T(8,128)S(1)}, f32[2,4,64,128]{3,2,1,0:T(8,128)S(1)}, u32[]{:S(2)}, u32[]{:S(2)}) collective-permute-start(f32[2,4,64,128]{3,2,1,0:T(8,128)S(1)} %get-tuple-element.25.refs_3_.first.refs_0_.refs_1_), channel_id=1, source_target_pairs={{0,8},{8,0},{16,24},{24,16},{1,9},{9,1},{17,25},{25,17},{2,10},{10... | collective-permute-start | bytes 786440 | tf_op jit(solution)/shard_map/ppermute | solution.py:417
  2.6 12.2 %collective-permute-start.6 = (f32[2,4,64,128]{3,2,1,0:T(8,128)S(1)}, f32[2,4,64,128]{3,2,1,0:T(8,128)S(1)}, u32[]{:S(2)}, u32[]{:S(2)}) collective-permute-start(f32[2,4,64,128]{3,2,1,0:T(8,128)S(1)} %get-tuple-element.24.refs_0_.refs_4_.fourth.refs_2_.refs_6_), channel_id=1, source_target_pairs={{0,8},{8,0},{16,24},{24,16},{1,9},{9,1},{17,25},{25,17},{2,10},{10... | collective-permute-start | bytes 786440 | tf_op jit(solution)/shard_map/ppermute | solution.py:417
  10.3 11.0 %collective-permute-start.9 = (f32[2,4,64,128]{3,2,1,0:T(8,128)S(1)}, f32[2,4,64,128]{3,2,1,0:T(8,128)S(1)}, u32[]{:S(2)}, u32[]{:S(2)}) collective-permute-start(f32[2,4,64,128]{3,2,1,0:T(8,128)S(1)} %collective-permute-done.8.refs_4_.refs_2_.refs_1_), channel_id=1, source_target_pairs={{0,16},{8,24},{16,0},{24,8},{1,17},{9,25},{17,1},{25,9},{2,18},{10... | collective-permute-start | bytes 786440 | tf_op jit(solution)/shard_map/ppermute | solution.py:422
  14.8 7.5 %collective-permute-start.7 = (f32[2,4,64,128]{3,2,1,0:T(8,128)S(1)}, f32[2,4,64,128]{3,2,1,0:T(8,128)S(1)}, u32[]{:S(2)}, u32[]{:S(2)}) collective-permute-start(f32[2,4,64,128]{3,2,1,0:T(8,128)S(1)} %collective-permute-done.6.refs_1_.refs_5_.refs_3_), channel_id=1, source_target_pairs={{0,16},{8,24},{16,0},{24,8},{1,17},{9,25},{17,1},{25,9},{2,18},{10... | collective-permute-start | bytes 786440 | tf_op jit(solution)/shard_map/ppermute | solution.py:422
  17.7 9.2 %collective-permute-start.16 = (f32[2,4,64,128]{3,2,1,0:T(8,128)S(1)}, f32[2,4,64,128]{3,2,1,0:T(8,128)S(1)}, u32[]{:S(2)}, u32[]{:S(2)}) collective-permute-start(f32[2,4,64,128]{3,2,1,0:T(8,128)S(1)} %get-tuple-element.31.second.refs_1_.refs_3_.refs_0_.refs_2_), channel_id=1, source_target_pairs={{0,8},{8,0},{16,24},{24,16},{1,9},{9,1},{17,25},{25,17},{2,10},{10... | collective-permute-start | bytes 786440 | tf_op jit(solution)/shard_map/ppermute | solution.py:417
  19.3 13.3 %collective-permute-start.14 = (f32[2,4,64,128]{3,2,1,0:T(8,128)S(1)}, f32[2,4,64,128]{3,2,1,0:T(8,128)S(1)}, u32[]{:S(2)}, u32[]{:S(2)}) collective-permute-start(f32[2,4,64,128]{3,2,1,0:T(8,128)S(1)} %get-tuple-element.34.refs_2_.refs_0_.refs_4_), channel_id=1, source_target_pairs={{0,8},{8,0},{16,24},{24,16},{1,9},{9,1},{17,25},{25,17},{2,10},{10... | collective-permute-start | bytes 786440 | tf_op jit(solution)/shard_map/ppermute | solution.py:417
  19.8 18.4 %collective-permute-start.12 = (f32[2,4,64,128]{3,2,1,0:T(8,128)S(1)}, f32[2,4,64,128]{3,2,1,0:T(8,128)S(1)}, u32[]{:S(2)}, u32[]{:S(2)}) collective-permute-start(f32[2,4,64,128]{3,2,1,0:T(8,128)S(1)} %get-tuple-element.27.refs_0_.refs_3_.refs_2_.refs_4_), channel_id=1, source_target_pairs={{0,8},{8,0},{16,24},{24,16},{1,9},{9,1},{17,25},{25,17},{2,10},{10... | collective-permute-start | bytes 786440 | tf_op jit(solution)/shard_map/ppermute | solution.py:417
  22.4 57.3 %collective-permute-start.10 = (f32[6,4,64,128]{3,2,1,0:T(8,128)S(1)}, f32[6,4,64,128]{3,2,1,0:T(8,128)S(1)}, u32[]{:S(2)}, u32[]{:S(2)}) collective-permute-start(f32[6,4,64,128]{3,2,1,0:T(8,128)S(1)} %get-tuple-element.26), channel_id=1, source_target_pairs={{1,0},{2,1},{3,2},{4,3},{5,4},{6,5},{7,6},{9,8},{10,9},{11,10},{12... | collective-permute-start | bytes 2359304 | tf_op jit(solution)/shard_map/ppermute | solution.py:432
  24.3 55.4 %collective-permute-start.11 = (f32[6,4,64,128]{3,2,1,0:T(8,128)S(1)}, f32[6,4,64,128]{3,2,1,0:T(8,128)S(1)}, u32[]{:S(2)}, u32[]{:S(2)}) collective-permute-start(f32[6,4,64,128]{3,2,1,0:T(8,128)S(1)} %get-tuple-element.30), channel_id=1, source_target_pairs={{0,1},{1,2},{2,3},{3,4},{4,5},{5,6},{6,7},{8,9},{9,10},{10,11},{11... | collective-permute-start | bytes 2359304 | tf_op jit(solution)/shard_map/ppermute | solution.py:427
  26.9 16.9 %collective-permute-start = (f32[2,4,64,128]{3,2,1,0:T(8,128)S(1)}, f32[2,4,64,128]{3,2,1,0:T(8,128)S(1)}, u32[]{:S(2)}, u32[]{:S(2)}) collective-permute-start(f32[2,4,64,128]{3,2,1,0:T(8,128)S(1)} %get-tuple-element.21.refs_1_.refs_0_.refs_2_.refs_4_), channel_id=1, source_target_pairs={{0,8},{8,0},{16,24},{24,16},{1,9},{9,1},{17,25},{25,17},{2,10},{10... | collective-permute-start | bytes 786440 | tf_op jit(solution)/shard_map/ppermute | solution.py:417
  32.6 16.9 %collective-permute-start.2 = (f32[2,4,64,128]{3,2,1,0:T(8,128)S(1)}, f32[2,4,64,128]{3,2,1,0:T(8,128)S(1)}, u32[]{:S(2)}, u32[]{:S(2)}) collective-permute-start(f32[2,4,64,128]{3,2,1,0:T(8,128)S(1)} %get-tuple-element.22.refs_2_.refs_0_.refs_4_), channel_id=1, source_target_pairs={{0,8},{8,0},{16,24},{24,16},{1,9},{9,1},{17,25},{25,17},{2,10},{10... | collective-permute-start | bytes 786440 | tf_op jit(solution)/shard_map/ppermute | solution.py:417
  38.2 14.6 %collective-permute-start.4 = (f32[2,4,64,128]{3,2,1,0:T(8,128)S(1)}, f32[2,4,64,128]{3,2,1,0:T(8,128)S(1)}, u32[]{:S(2)}, u32[]{:S(2)}) collective-permute-start(f32[2,4,64,128]{3,2,1,0:T(8,128)S(1)} %get-tuple-element.23.refs_3_.refs_4_.refs_2_.third.refs_0_), channel_id=1, source_target_pairs={{0,8},{8,0},{16,24},{24,16},{1,9},{9,1},{17,25},{25,17},{2,10},{10... | collective-permute-start | bytes 786440 | tf_op jit(solution)/shard_map/ppermute | solution.py:417
  43.8 9.5 %collective-permute-start.17 = (f32[2,4,64,128]{3,2,1,0:T(8,128)S(1)}, f32[2,4,64,128]{3,2,1,0:T(8,128)S(1)}, u32[]{:S(2)}, u32[]{:S(2)}) collective-permute-start(f32[2,4,64,128]{3,2,1,0:T(8,128)S(1)} %collective-permute-done.16.refs_4_.refs_1_.refs_3_), channel_id=1, source_target_pairs={{0,16},{8,24},{16,0},{24,8},{1,17},{9,25},{17,1},{25,9},{2,18},{10... | collective-permute-start | bytes 786440 | tf_op jit(solution)/shard_map/ppermute | solution.py:422
  49.4 9.0 %collective-permute-start.15 = (f32[2,4,64,128]{3,2,1,0:T(8,128)S(1)}, f32[2,4,64,128]{3,2,1,0:T(8,128)S(1)}, u32[]{:S(2)}, u32[]{:S(2)}) collective-permute-start(f32[2,4,64,128]{3,2,1,0:T(8,128)S(1)} %collective-permute-done.14.refs_1_.refs_3_.refs_5_), channel_id=1, source_target_pairs={{0,16},{8,24},{16,0},{24,8},{1,17},{9,25},{17,1},{25,9},{2,18},{10... | collective-permute-start | bytes 786440 | tf_op jit(solution)/shard_map/ppermute | solution.py:422
  52.8 11.2 %collective-permute-start.13 = (f32[2,4,64,128]{3,2,1,0:T(8,128)S(1)}, f32[2,4,64,128]{3,2,1,0:T(8,128)S(1)}, u32[]{:S(2)}, u32[]{:S(2)}) collective-permute-start(f32[2,4,64,128]{3,2,1,0:T(8,128)S(1)} %collective-permute-done.12.refs_1_.refs_3_.refs_5_), channel_id=1, source_target_pairs={{0,16},{8,24},{16,0},{24,8},{1,17},{9,25},{17,1},{25,9},{2,18},{10... | collective-permute-start | bytes 786440 | tf_op jit(solution)/shard_map/ppermute | solution.py:422
  53.3 32.3 %collective-permute-start.1 = (f32[2,4,64,128]{3,2,1,0:T(8,128)S(1)}, f32[2,4,64,128]{3,2,1,0:T(8,128)S(1)}, u32[]{:S(2)}, u32[]{:S(2)}) collective-permute-start(f32[2,4,64,128]{3,2,1,0:T(8,128)S(1)} %collective-permute-done.refs_1_.refs_3_.refs_5_), channel_id=1, source_target_pairs={{0,16},{8,24},{16,0},{24,8},{1,17},{9,25},{17,1},{25,9},{2,18},{10... | collective-permute-start | bytes 786440 | tf_op jit(solution)/shard_map/ppermute | solution.py:422
  58.4 29.4 %collective-permute-start.3 = (f32[2,4,64,128]{3,2,1,0:T(8,128)S(1)}, f32[2,4,64,128]{3,2,1,0:T(8,128)S(1)}, u32[]{:S(2)}, u32[]{:S(2)}) collective-permute-start(f32[2,4,64,128]{3,2,1,0:T(8,128)S(1)} %collective-permute-done.2.refs_3_.refs_1_.refs_5_), channel_id=1, source_target_pairs={{0,16},{8,24},{16,0},{24,8},{1,17},{9,25},{17,1},{25,9},{2,18},{10... | collective-permute-start | bytes 786440 | tf_op jit(solution)/shard_map/ppermute | solution.py:422
  64.0 26.1 %collective-permute-start.5 = (f32[2,4,64,128]{3,2,1,0:T(8,128)S(1)}, f32[2,4,64,128]{3,2,1,0:T(8,128)S(1)}, u32[]{:S(2)}, u32[]{:S(2)}) collective-permute-start(f32[2,4,64,128]{3,2,1,0:T(8,128)S(1)} %collective-permute-done.4.refs_5_.refs_3_.refs_1_), channel_id=1, source_target_pairs={{0,16},{8,24},{16,0},{24,8},{1,17},{9,25},{17,1},{25,9},{2,18},{10... | collective-permute-start | bytes 786440 | tf_op jit(solution)/shard_map/ppermute | solution.py:422
where the time goes:
time: 96 us; the launch traced here: 94.9 us
  waiting for transfers between devices  40.4 us (42%)
  Pallas kernels  32.6 us (34%)
  starting transfers between devices  21.6 us (22%)
    ppermute x8, waiting for transfers between devices, across(): return lax.ppermute(value, 'phase', [(q, q ^ 1) for q in range(n)])  30.7 us
    pallas_call x6, Pallas kernels, last_side(): pl.pallas_call(functools.partial(last_kernel, js, count, [bases[j] for j...  15.5 us
    ppermute x8, starting transfers between devices, across(): return lax.ppermute(value, 'phase', [(q, q ^ 1) for q in range(n)])  10.1 us
    ppermute x8, waiting for transfers between devices, onward(): lax.ppermute(value, 'phase', [(q, (q + (2 if q % 2 == 0 else n - 2)) % n)...  9.68 us
    pallas_call x8, Pallas kernels, first_side(): pl.pallas_call(functools.partial(first_kernel, j, count, base, tuple(want...  8.54 us
    ppermute x8, starting transfers between devices, onward(): lax.ppermute(value, 'phase', [(q, (q + (2 if q % 2 == 0 else n - 2)) % n)...  7.09 us
    pallas_call x2, Pallas kernels, own_inner(): pl.pallas_call(functools.partial(own_inner_kernel, size), out_shape=(shap...  4.43 us
    pallas_call x2, Pallas kernels, cut_blocks(): pl.pallas_call(functools.partial(cut_kernel, bs), out_shape=[like(phases,...  2.44 us
  transfers between devices with their start and end apart: 18, of which 11 were waited for; matrix products, arithmetic and copies ran while one was open for 0% of the time, Pallas kernels for 28%

commit v1 on v0

v1 whole, which is shorter than its diff:
```python
import functools

import jax
import jax.numpy as jnp
from jax import lax
from jax.experimental import pallas as pl
from jax.experimental.pallas import tpu as pltpu
from jax.sharding import PartitionSpec as P


EPSILON = 1e-05
CELLS = 729.0
BLOCK = 4
GROUPS = {5: ((0, 1, 2), (3, 4)), 7: ((0, 1, 2), (3, 4), (5, 6))}
VMEM = pl.BlockSpec(memory_space=pltpu.VMEM)
ANY = pl.BlockSpec(memory_space=pl.ANY)
GRANT = 12


def box_matrix(width):
    i = lax.broadcasted_iota(jnp.int32, (width, width), 0)
    j = lax.broadcasted_iota(jnp.int32, (width, width), 1)
    return jnp.where(jnp.abs(i - j) <= 4, 1.0, 0.0).astype(jnp.bfloat16)


def thirds(v):
    high = v.astype(jnp.bfloat16)
    rest = v - high.astype(jnp.float32)
    middle = rest.astype(jnp.bfloat16)
    low = (rest - middle.astype(jnp.float32)).astype(jnp.bfloat16)
    return high, middle, low


def depth_sums(read, planes):
    sums = []
    while len(sums) < planes:
        base = len(sums)
        if planes - base >= 8:
            back = [read(base + 7)]
            for k in range(6, -1, -1):
                back.append(back[-1] + read(base + k))
            ahead = read(base + 8)
            sums.append(back[7] + ahead)
            for k in range(1, 8):
                ahead = ahead + read(base + 8 + k)
                sums.append(back[7 - k] + ahead)
        else:
            p = [read(base + k) for k in range(12)]
            core = ((p[3] + p[4]) + (p[5] + p[6])) + (p[7] + p[8])
            a = p[1] + p[2]
            b = p[9] + p[10]
            sums += [core + (p[0] + a), core + (a + p[9]), core + (p[2] + b), core + (b + p[11])]
    return sums


def clear_rims(tz, rows):
    zero = jnp.zeros((8, tz.shape[-1]), jnp.float32)
    for w in range(tz.shape[0]):
        for i in range(tz.shape[1]):
            tz[w, i, 0:8, :] = zero
            tz[w, i, rows + 8 : rows + 16, :] = zero


def plane_sums(i, tz, t3, sx, box):
    windows, rows = tz.shape[0], tz.shape[2] - 16
    e = i % BLOCK
    for w in range(windows):
        for r in range(0, rows + 8, 8):
            t3[e, w, r : r + 8, :] = (
                tz[w, i, r + 3 : r + 11, :] + tz[w, i, r + 4 : r + 12, :] + tz[w, i, r + 5 : r + 13, :]
            )
    for group in GROUPS[windows]:
        parts = [
            thirds(t3[e, w, 1 : rows + 1, :] + t3[e, w, 4 : rows + 4, :] + t3[e, w, 7 : rows + 7, :]) for w in group
        ]
        sums = None
        for t in range(3):
            term = jnp.dot(
                jnp.concatenate([p[t] for p in parts], axis=0), box, preferred_element_type=jnp.float32
            )
            sums = term if sums is None else sums + term
        for k, w in enumerate(group):
            sx[w, e] = sums[rows * k : rows * (k + 1)]


def pair_weight(s_both, s_a, m_b, v_a, v_b):
    c = s_both - s_a * m_b
    return c, c / (v_a * v_b + EPSILON * CELLS * CELLS)


def row_blocks(rows, body):
    @pl.loop(0, rows // 16)
    def _(y):
        for half in range(2):
            r = pl.multiple_of(y * 16 + 8 * half, 8)
            body(pl.ds(r, 8), pl.ds(pl.multiple_of(r + 8, 8), 8))


def plane_of(parts, base):
    def read(a, p, rows):
        z = base + p
        for ref, offset, first, length in parts:
            if first <= z < first + length:
                return ref[a + offset, z - first, rows, :]
        raise ValueError("plane")

    return read


def own_block(read, stats, acc, z_out, tz, t3, sx, box):
    rows = tz.shape[2] - 16

    def body(here, there):
        zero = [read(0, p, here) for p in range(3 * BLOCK)]
        one = [read(1, p, here) for p in range(3 * BLOCK)]
        terms = [
            lambda p: zero[p],
            lambda p: zero[p] * zero[p],
            lambda p: one[p],
            lambda p: one[p] * one[p],
            lambda p: zero[p] * one[p],
        ]
        for w, term in enumerate(terms):
            for i, v in enumerate(depth_sums(term, BLOCK)):
                tz[w, i, there, :] = v

    row_blocks(rows, body)

    for i in range(BLOCK):
        plane_sums(i, tz, t3, sx, box)
        for y in range(0, rows, 8):
            r = slice(y, y + 8)
            s_0, q_0, s_1, q_1, both = [sx[w, i, r, :] for w in range(5)]
            m_0, m_1 = s_0 * (1.0 / CELLS), s_1 * (1.0 / CELLS)
            v_0 = q_0 - s_0 * m_0
            v_1 = q_1 - s_1 * m_1
            c, g = pair_weight(both, s_0, m_1, v_0, v_1)
            z = z_out + i
            stats[0, 0, z, r, :] = s_0
            stats[0, 1, z, r, :] = v_0
            stats[1, 0, z, r, :] = s_1
            stats[1, 1, z, r, :] = v_1
            acc[0, 0, z, r, :] = g * (read(1, BLOCK + i, r) - m_1)
            acc[1, 0, z, r, :] = g * (read(0, BLOCK + i, r) - m_0)
            gc = g * c
            acc[0, 1, z, r, :] = gc
            acc[1, 1, z, r, :] = gc


def own_inner_kernel(size, *refs):
    parts, (stats, acc, field, tz, t3, sx) = refs[: size + 2], refs[size + 2 :]
    rows, width = parts[0].shape[2:]
    clear_rims(tz, rows)
    box = box_matrix(width)
    for k, part in enumerate(parts):
        for a in range(2):
            field[a, BLOCK * k : BLOCK * (k + 1)] = part[a]

    @pl.loop(0, size)
    def _(j):
        own_block(lambda a, p, rows: field[a, BLOCK * j + p, rows, :], stats, acc, BLOCK * j, tz, t3, sx, box)


def own_ends_kernel(low, high, first, second, third, fourth, stats, acc, field, tz, t3, sx):
    rows, width = first.shape[2:]
    clear_rims(tz, rows)
    box = box_matrix(width)
    for e, parts in enumerate(((low, first, second), (third, fourth, high))):
        for k, part in enumerate(parts):
            for a in range(2):
                field[e, a, BLOCK * k : BLOCK * (k + 1)] = part[a]

    @pl.loop(0, 2)
    def _(e):
        own_block(lambda a, p, rows: field[e, a, p, rows, :], stats, acc, BLOCK * e, tz, t3, sx, box)


def side_group(planes, near, own, theirs, tables, tz, t3, sx, box, sink, done):
    rows = tz.shape[2] - 16
    far = 1 - near
    own_near, own_far = far, near

    def body(here, there):
        def n(p):
            return theirs(near, p, here)

        def f(p):
            return theirs(far, p, here)

        def square(read):
            def term(p):
                v = read(p)
                return v * v

            return term

        terms = [
            n,
            square(n),
            lambda p: n(p) * own(own_near, p, here),
            lambda p: n(p) * own(own_far, p, here),
            f,
            square(f),
            lambda p: f(p) * own(own_near, p, here),
        ]
        for w, term in enumerate(terms):
            for i, v in enumerate(depth_sums(term, planes)):
                tz[w, i, there, :] = v

    row_blocks(rows, body)

    for i in range(planes):
        plane_sums(i, tz, t3, sx, box)
        stats, z, acc, b = tables(i)
        for y in range(0, rows, 8):
            r = slice(y, y + 8)
            s_n, q_n, nn, fn, s_f, q_f, nf = [sx[w, i % BLOCK, r, :] for w in range(7)]
            o_s, o_v = stats[own_near, 0, z, r, :], stats[own_near, 1, z, r, :]
            p_s, p_v = stats[own_far, 0, z, r, :], stats[own_far, 1, z, r, :]
            m_n, m_f = s_n * (1.0 / CELLS), s_f * (1.0 / CELLS)
            v_n = q_n - s_n * m_n
            v_f = q_f - s_f * m_f
            off_n = theirs(near, BLOCK + i, r) - m_n
            off_f = theirs(far, BLOCK + i, r) - m_f
            c_nn, g_nn = pair_weight(nn, o_s, m_n, o_v, v_n)
            c_nf, g_nf = pair_weight(nf, o_s, m_f, o_v, v_f)
            c_fn, g_fn = pair_weight(fn, p_s, m_n, p_v, v_n)
            sink(own_near, i, r, acc[own_near, 0, b, r, :] + g_nn * off_n + g_nf * off_f,
                 acc[own_near, 1, b, r, :] + g_nn * c_nn + g_nf * c_nf, o_s, o_v)
            sink(own_far, i, r, acc[own_far, 0, b, r, :] + g_fn * off_n,
                 acc[own_far, 1, b, r, :] + g_fn * c_fn, p_s, p_v)
        done(i)


def readers(j, count, rims, refs):
    depth = BLOCK * count
    own = [(ref, 0, BLOCK * k[1], BLOCK) for k, ref in refs.items() if k[0] == "own"]
    theirs = [(ref, 0, BLOCK * k[1], BLOCK) for k, ref in refs.items() if k[0] == "side"]
    for name, first in (("low", -BLOCK), ("high", depth)):
        if (name,) in refs:
            own.append((refs[name,], 0, first, BLOCK))
            theirs.append((refs[name + rims[0],], rims[1], first, BLOCK))
    base = BLOCK * (j - 1)
    return plane_of(own, base), plane_of(theirs, base)


def split_refs(keys, refs):
    return dict(zip(keys, refs[: len(keys)])), refs[len(keys) :]


def first_kernel(js, count, bases, keys, *refs):
    refs, (out, tz, t3, sx) = split_refs(keys, refs)
    near = lax.rem(lax.axis_index("phase"), 2)
    rows, width = refs["own", js[0]].shape[2:]
    clear_rims(tz, rows)
    own, theirs = readers(js[0], count, ("", 2), refs)

    def tables(i):
        j, z = js[i // BLOCK], bases[i // BLOCK] + i % BLOCK
        return refs["stats", j], z, refs["acc", j], z

    def sink(a, i, r, one, two, s, v):
        out[a, 0, i, r, :] = one
        out[a, 1, i, r, :] = two

    side_group(BLOCK * len(js), near, own, theirs, tables, tz, t3, sx, box_matrix(width), sink, lambda i: None)


def last_kernel(js, count, bases, sums_base, before, final, keys, *refs):
    refs, rest = split_refs(keys, refs)
    if before is not None:
        out, rest = rest[0], rest[1:]
    if not final:
        block, rest = rest[0], rest[1:]
    tz, t3, sx, coef, padded, *rest = rest
    if final:
        block, rest = rest[0], rest[1:]
    planes = BLOCK * len(js)
    first = BLOCK * js[0]
    copies = []

    def write(source, first, sem):
        copy = pltpu.make_async_copy(source, out.at[:, :, first : first + source.shape[2]], sem)
        copy.start()
        copies.append(copy)

    if before is not None:
        sems = rest[0]
        write(refs["block",], BLOCK * before, sems.at[0])
    near = 1 - lax.rem(lax.axis_index("phase"), 2)
    rows, width = refs["own", js[0]].shape[2:]
    clear_rims(tz, rows)
    zero = jnp.zeros((8, width), jnp.float32)
    for a in range(2):
        padded[a, 0:8, :] = zero
        padded[a, rows + 8 : rows + 16, :] = zero
    lane = lax.broadcasted_iota(jnp.int32, (8, width), 1)
    own, theirs = readers(js[0], count, ("_b", 0), refs)

    def tables(i):
        j = js[i // BLOCK]
        return refs["stats", j], bases[i // BLOCK] + i % BLOCK, refs["acc", j], sums_base[i // BLOCK] + i % BLOCK

    def sink(a, i, r, one, two, s, v):
        here = own(a, BLOCK + i, r) - s * (1.0 / CELLS)
        coef[a, i % BLOCK, r, :] = CELLS * (one - two / (v + EPSILON * CELLS) * here)

    def forces(i):
        for a in range(2):
            padded[a, 8 : rows + 8, :] = own(a, BLOCK + i, slice(0, rows))
            for y in range(0, rows, 8):
                r = slice(y, y + 8)
                c = coef[a, i % BLOCK, r, :]
                block[0, a, i, r, :] = c * (own(a, i + 5, r) - own(a, i + 3, r))
                block[1, a, i, r, :] = c * (padded[a, y + 9 : y + 17, :] - padded[a, y + 7 : y + 15, :])
                v = padded[a, y + 8 : y + 16, :]
                after_x = jnp.where(lane < width - 1, pltpu.roll(v, width - 1, 1), 0.0)
                before_x = jnp.where(lane > 0, pltpu.roll(v, 1, 1), 0.0)
                block[2, a, i, r, :] = c * (after_x - before_x)

    starts = [0] + [i for i in range(BLOCK, planes, BLOCK)] + [planes - 2, planes]

    def done(i):
        if i + 1 in starts:
            low = max(k for k in starts if k <= i)
            for k in range(low, i + 1):
                forces(k)
            if final:
                write(block.at[:, :, low : i + 1], first + low, sems.at[1 + starts.index(low)])

    side_group(planes, near, own, theirs, tables, tz, t3, sx, box_matrix(width), sink, done)
    for copy in copies:
        copy.wait()


def scratches(windows, rows, width, blocks=1):
    return [
        pltpu.VMEM((windows, BLOCK * blocks, rows + 16, width), jnp.float32),
        pltpu.VMEM((BLOCK, windows, rows + 8, width), jnp.float32),
        pltpu.VMEM((windows, BLOCK, rows, width), jnp.float32),
    ]


def params(mib=GRANT):
    return pltpu.CompilerParams(vmem_limit_bytes=mib << 20)


def like(*shape):
    return jax.ShapeDtypeStruct(shape, jnp.float32)


def cut_kernel(bs, images, *refs):
    outs, sems = refs[:-1], refs[-1]
    copies = [
        pltpu.make_async_copy(images.at[:, BLOCK * b : BLOCK * (b + 1)], outs[n], sems.at[n]) for n, b in enumerate(bs)
    ]
    for copy in copies:
        copy.start()
    for copy in copies:
        copy.wait()


def cut_blocks(bs, images, mib):
    phases, _, rows, width = images.shape
    outs = pl.pallas_call(
        functools.partial(cut_kernel, bs),
        out_shape=[like(phases, BLOCK, rows, width)] * len(bs),
        in_specs=[pl.BlockSpec(memory_space=pltpu.HBM)],
        out_specs=[VMEM] * len(bs),
        scratch_shapes=[pltpu.SemaphoreType.DMA((len(bs),))],
        compiler_params=params(mib),
    )(pltpu.with_memory_space_constraint(images, pltpu.HBM))
    return dict(zip(bs, outs))


def pack_kernel(*refs):
    for n in range(2):
        for k in range(2):
            for a in range(2):
                refs[4 + n][2 * k + a] = refs[2 * n + k][a]


def packed(groups):
    shape = groups[0][0].shape
    out = like(2 * shape[0], *shape[1:])
    return pl.pallas_call(
        pack_kernel,
        out_shape=(out, out),
        in_specs=[VMEM] * 4,
        out_specs=(VMEM, VMEM),
        compiler_params=params(6),
        name="pack",
    )(*groups[0], *groups[1])


def own_inner(low, high, blocks):
    rows, width = blocks[low].shape[2:]
    size = high - low
    shape = like(2, 2, BLOCK * size, rows, width)
    return pl.pallas_call(
        functools.partial(own_inner_kernel, size),
        out_shape=(shape, shape),
        in_specs=[VMEM] * (size + 2),
        out_specs=(VMEM, VMEM),
        scratch_shapes=[pltpu.VMEM((2, BLOCK * (size + 2), rows, width), jnp.float32)] + scratches(5, rows, width),
        compiler_params=params(),
    )(*[blocks[b] for b in range(low - 1, high + 1)])


def own_ends(low, high, *blocks):
    rows, width = low.shape[2:]
    shape = like(2, 2, 2 * BLOCK, rows, width)
    return pl.pallas_call(
        own_ends_kernel,
        out_shape=(shape, shape),
        in_specs=[VMEM] * 6,
        out_specs=(VMEM, VMEM),
        scratch_shapes=[pltpu.VMEM((2, 2, 3 * BLOCK, rows, width), jnp.float32)] + scratches(5, rows, width),
        compiler_params=params(),
        name="own_ends",
    )(low, high, *blocks)


def gather_operands(js, count, own, side, rims):
    wanted = {}
    for b in range(js[0] - 1, js[-1] + 2):
        if 0 <= b < count:
            wanted["own", b] = own[b]
            wanted["side", b] = side[b]
        else:
            for name in rims:
                if name.startswith("low" if b < 0 else "high"):
                    wanted[name,] = rims[name]
    return wanted


def specs_of(wanted):
    return [ANY if k == ("forces",) else VMEM for k in wanted]


def first_side(js, count, own, side, rims, stats, accs, bases):
    rows, width = own[0].shape[2:]
    wanted = gather_operands(js, count, own, side, rims)
    for j in js:
        wanted["stats", j], wanted["acc", j] = stats[j], accs[j]
    return pl.pallas_call(
        functools.partial(first_kernel, js, count, [bases[j] for j in js], tuple(wanted)),
        out_shape=like(2, 2, BLOCK * len(js), rows, width),
        in_specs=specs_of(wanted),
        out_specs=VMEM,
        scratch_shapes=scratches(7, rows, width, len(js)),
        compiler_params=params(),
    )(*wanted.values())


def last_side(js, count, own, side, rims, stats, bases, sums, before, block, forces, final):
    rows, width = own[0].shape[2:]
    wanted = gather_operands(js, count, own, side, rims)
    for j in js:
        wanted["stats", j], wanted["acc", j] = stats[j], sums[j][0]
    if before is not None:
        wanted["block",] = block
    if forces is not None:
        wanted["forces",] = forces
    whole = like(3, 2, BLOCK * count, rows, width)
    piece = (3, 2, BLOCK * len(js), rows, width)
    outs = ([(whole, ANY)] if before is not None else []) + ([] if final else [(like(*piece), VMEM)])
    got = pl.pallas_call(
        functools.partial(
            last_kernel, js, count, [bases[j] for j in js], [sums[j][1] for j in js], before, final, tuple(wanted)
        ),
        out_shape=[shape for shape, _ in outs],
        in_specs=specs_of(wanted),
        out_specs=[spec for _, spec in outs],
        input_output_aliases={len(wanted) - 1: 0} if forces is not None else {},
        scratch_shapes=scratches(7, rows, width, len(js))
        + [pltpu.VMEM((2, BLOCK, rows, width), jnp.float32), pltpu.VMEM((2, rows + 16, width), jnp.float32)]
        + ([pltpu.VMEM(piece, jnp.float32)] if final else [])
        + ([pltpu.SemaphoreType.DMA((2 + len(js) if final else 1,))] if before is not None else []),
        compiler_params=params(),
    )(*wanted.values())
    forces = got[0] if before is not None else None
    return forces, None if final else got[-1]


def across(value):
    n = lax.axis_size("phase")
    return lax.ppermute(value, "phase", [(q, q ^ 1) for q in range(n)])


def onward(value):
    n = lax.axis_size("phase")
    return lax.ppermute(value, "phase", [(q, (q + (2 if q % 2 == 0 else n - 2)) % n) for q in range(n)])


def yonder(value):
    n = lax.axis_size("phase")
    return lax.ppermute(value, "phase", [(q, (q + (n - 2 if q % 2 == 0 else 2)) % n) for q in range(n)])


def upward(value):
    n = lax.axis_size("slab")
    return lax.ppermute(value, "slab", [(q, q + 1) for q in range(n - 1)])


def downward(value):
    n = lax.axis_size("slab")
    return lax.ppermute(value, "slab", [(q + 1, q) for q in range(n - 1)])


def local_forces(images):
    count = images.shape[1] // BLOCK
    assert images.shape[0] == 2 and images.shape[1] == BLOCK * count and count >= 6
    assert lax.axis_size("phase") % 2 == 0
    half = (count + 1) // 2

    top, end, turned = 0, count - 1, count - 2
    blocks = cut_blocks((top,), images, 4)
    blocks.update(cut_blocks((end, turned), images, 4))
    blocks.update(cut_blocks(tuple(range(1, turned)), images, 4))
    one = {b: across(blocks[b]) for b in blocks}
    two = {b: onward(one[b]) for b in blocks if b != turned}
    two[turned] = across(yonder(blocks[turned]))
    low, high = packed([(blocks[end], one[end]), (blocks[top], one[top])])
    rims = {"low": upward(low), "high": downward(high), "low_b": upward(two[end]), "high_b": downward(two[top])}

    near_half = own_inner(1, half, blocks)
    far_half = own_inner(half, count - 1, blocks)
    outer = own_ends(rims["low"], rims["high"], blocks[0], blocks[1], blocks[end - 1], blocks[end])
    stats, acc, base = {}, {}, {}
    for j in range(count):
        if j in (0, count - 1):
            (stats[j], acc[j]), base[j] = outer, 0 if j == 0 else BLOCK
        elif j < half:
            (stats[j], acc[j]), base[j] = near_half, BLOCK * (j - 1)
        else:
            (stats[j], acc[j]), base[j] = far_half, BLOCK * (j - half)
    shared = {name: rims[name] for name in ("low", "high")}
    sums = {}
    for js in first_groups(count):
        total = first_side(js, count, blocks, one, shared, stats, acc, base)
        sums.update({j: (total, BLOCK * k) for k, j in enumerate(js)})
    forces, block, before = None, None, None
    groups = last_groups(count)
    for js in groups:
        forces, block = last_side(
            js, count, blocks, two, rims, stats, base, sums, before, block, forces, js == groups[-1]
        )
        before = js[0]
    return forces


def first_groups(count):
    return [(j,) for j in range(count - 3)] + [tuple(range(count - 3, count))]


def last_groups(count):
    return [(j,) for j in range(count - 3)] + [tuple(range(count - 3, count))]


def solution(mesh):
    in_specs = (P("phase", "slab", None, None),)
    out_specs = P(None, "phase", "slab", None, None)
    return jax.shard_map(local_forces, mesh=mesh, in_specs=in_specs, out_specs=out_specs, check_vma=False)
```

time: 96 us -> 99.6 us (1.037)
  starting transfers between devices: 21.6 us -> 29.5 us
  Pallas kernels: 32.6 us -> 26.7 us
    pallas_call x6, Pallas kernels: 15.5 us -> 10.2 us  [last_side(): pl.pallas_call(functools.partial(last_kernel, js, count, [bases[j] for j...]
    ppermute x8 -> x7, waiting for transfers between devices: 9.68 us -> 13.4 us  [onward(): lax.ppermute(value, 'phase', [(q, (q + (2 if q % 2 == 0 else n - 2)) % n)...]
    ppermute x8 -> x9, waiting for transfers between devices: 30.7 us -> 27.9 us  [across(): return lax.ppermute(value, 'phase', [(q, q ^ 1) for q in range(n)])]
    ppermute x1 -> x2, starting transfers between devices: 1.92 us -> 3.82 us  [downward(): return lax.ppermute(value, 'slab', [(q + 1, q) for q in range(n - 1)])]
    ppermute x8 -> x9, starting transfers between devices: 10.1 us -> 11.7 us  [across(): return lax.ppermute(value, 'phase', [(q, q ^ 1) for q in range(n)])]
    ppermute x8 -> x7, starting transfers between devices: 7.09 us -> 8.61 us  [onward(): lax.ppermute(value, 'phase', [(q, (q + (2 if q % 2 == 0 else n - 2)) % n)...]
    ppermute x0 -> x1, starting transfers between devices: none -> 1.52 us  [yonder(): lax.ppermute(value, 'phase', [(q, (q + (n - 2 if q % 2 == 0 else 2)) % n)...]
    ppermute x1 -> x2, starting transfers between devices: 2.41 us -> 3.82 us  [upward(): return lax.ppermute(value, 'slab', [(q, q + 1) for q in range(n - 1)])]
  transfers between devices with their start and end apart: 18 -> 21, of which waited for: 11 -> 11; matrix products, arithmetic and copies ran while one was open for 0% -> 0% of each run, Pallas kernels for 28% -> 22%
where the time goes in v1:
time: 99.6 us; the launch traced here: 97.9 us
  waiting for transfers between devices  41.3 us (41%)
  starting transfers between devices  29.5 us (30%)
  Pallas kernels  26.7 us (27%)
    ppermute x9, waiting for transfers between devices, across(): return lax.ppermute(value, 'phase', [(q, q ^ 1) for q in range(n)])  27.9 us
    ppermute x7, waiting for transfers between devices, onward(): lax.ppermute(value, 'phase', [(q, (q + (2 if q % 2 == 0 else n - 2)) % n)...  13.4 us
    ppermute x9, starting transfers between devices, across(): return lax.ppermute(value, 'phase', [(q, q ^ 1) for q in range(n)])  11.7 us
    pallas_call x6, Pallas kernels, last_side(): pl.pallas_call(functools.partial(last_kernel, js, count, [bases[j] for j...  10.2 us
    ppermute x7, starting transfers between devices, onward(): lax.ppermute(value, 'phase', [(q, (q + (2 if q % 2 == 0 else n - 2)) % n)...  8.61 us
    pallas_call x6, Pallas kernels, first_side(): pl.pallas_call(functools.partial(first_kernel, js, count, [bases[j] for j...  7.56 us
    pallas_call x2, Pallas kernels, own_inner(): pl.pallas_call(functools.partial(own_inner_kernel, size), out_shape=(shap...  4.11 us
    ppermute x2, starting transfers between devices, downward(): return lax.ppermute(value, 'slab', [(q + 1, q) for q in range(n - 1)])  3.82 us
  transfers between devices with their start and end apart: 21, of which 11 were waited for; matrix products, arithmetic and copies ran while one was open for 0% of the time, Pallas kernels for 22%

profile of v1, /device:TPU:16, one launch (start us, length us, event | category | flops | bytes accessed | tf_op | source)
XLA Modules:
  0.0 97.9 jit_solution(6297347743539074995)
XLA Ops:
  1.0 1.6 %collective-permute-start.8 = (f32[2,4,64,128]{3,2,1,0:T(8,128)S(1)}, f32[2,4,64,128]{3,2,1,0:T(8,128)S(1)}, u32[]{:S(2)}, u32[]{:S(2)}) collective-permute-start(f32[2,4,64,128]{3,2,1,0:T(8,128)S(1)} %shard_map.19.refs_2_.first.refs_0_.refs_1_), channel_id=1, source_target_pairs={{0,8},{8,0},{16,24},{24,16},{1,9},{9,1},{17,25},{25,17},{2,10},{10... | collective-permute-start | bytes 786440 | tf_op jit(solution)/shard_map/ppermute | solution.py:488
  5.5 1.6 %collective-permute-start.18 = (f32[2,4,64,128]{3,2,1,0:T(8,128)S(1)}, f32[2,4,64,128]{3,2,1,0:T(8,128)S(1)}, u32[]{:S(2)}, u32[]{:S(2)}) collective-permute-start(f32[2,4,64,128]{3,2,1,0:T(8,128)S(1)} %get-tuple-element.37.second.refs_1_.refs_0_.refs_2_.refs_3_.refs_4_), channel_id=1, source_target_pairs={{0,8},{8,0},{16,24},{24,16},{1,9},{9,1},{17,25},{25,17},{2,10},{10... | collective-permute-start | bytes 786440 | tf_op jit(solution)/shard_map/ppermute | solution.py:488
  11.7 4.1 %collective-permute-done.6.refs_1_.refs_7_ = f32[2,4,64,128]{3,2,1,0:T(8,128)S(1)} collective-permute-done((f32[2,4,64,128]{3,2,1,0:T(8,128)S(1)}, f32[2,4,64,128]{3,2,1,0:T(8,128)S(1)}, u32[]{:S(2)}, u32[]{:S(2)}) %collective-permute-start.6) | collective-permute-done | bytes 262176 | tf_op jit(solution)/shard_map/ppermute | solution.py:488
  17.3 4.1 %collective-permute-done.18.refs_1_.refs_3_.refs_4_ = f32[2,4,64,128]{3,2,1,0:T(8,128)S(1)} collective-permute-done((f32[2,4,64,128]{3,2,1,0:T(8,128)S(1)}, f32[2,4,64,128]{3,2,1,0:T(8,128)S(1)}, u32[]{:S(2)}, u32[]{:S(2)}) %collective-permute-start.18) | collective-permute-done | bytes 262176 | tf_op jit(solution)/shard_map/ppermute | solution.py:488
  22.9 4.1 %collective-permute-done.16.refs_1_.refs_3_.refs_5_ = f32[2,4,64,128]{3,2,1,0:T(8,128)S(1)} collective-permute-done((f32[2,4,64,128]{3,2,1,0:T(8,128)S(1)}, f32[2,4,64,128]{3,2,1,0:T(8,128)S(1)}, u32[]{:S(2)}, u32[]{:S(2)}) %collective-permute-start.16) | collective-permute-done | bytes 262176 | tf_op jit(solution)/shard_map/ppermute | solution.py:488
  28.6 4.1 %collective-permute-done.14.refs_1_.refs_3_.refs_5_ = f32[2,4,64,128]{3,2,1,0:T(8,128)S(1)} collective-permute-done((f32[2,4,64,128]{3,2,1,0:T(8,128)S(1)}, f32[2,4,64,128]{3,2,1,0:T(8,128)S(1)}, u32[]{:S(2)}, u32[]{:S(2)}) %collective-permute-start.14) | collective-permute-done | bytes 262176 | tf_op jit(solution)/shard_map/ppermute | solution.py:488
  32.7 1.5 %collective-permute-start.19 = (f32[2,4,64,128]{3,2,1,0:T(8,128)S(1)}, f32[2,4,64,128]{3,2,1,0:T(8,128)S(1)}, u32[]{:S(2)}, u32[]{:S(2)}) collective-permute-start(f32[2,4,64,128]{3,2,1,0:T(8,128)S(1)} %collective-permute-done.18.refs_1_.refs_3_.refs_4_), channel_id=1, source_target_pairs={{0,16},{8,24},{16,0},{24,8},{1,17},{9,25},{17,1},{25,9},{2,18},{10... | collective-permute-start | bytes 786440 | tf_op jit(solution)/shard_map/ppermute | solution.py:493
  34.3 4.0 %collective-permute-done.refs_1_.refs_3_.refs_5_ = f32[2,4,64,128]{3,2,1,0:T(8,128)S(1)} collective-permute-done((f32[2,4,64,128]{3,2,1,0:T(8,128)S(1)}, f32[2,4,64,128]{3,2,1,0:T(8,128)S(1)}, u32[]{:S(2)}, u32[]{:S(2)}) %collective-permute-start) | collective-permute-done | bytes 262176 | tf_op jit(solution)/shard_map/ppermute | solution.py:488
  38.3 1.9 %collective-permute-start.13 = (f32[4,4,64,128]{3,2,1,0:T(8,128)S(1)}, f32[4,4,64,128]{3,2,1,0:T(8,128)S(1)}, u32[]{:S(2)}, u32[]{:S(2)}) collective-permute-start(f32[4,4,64,128]{3,2,1,0:T(8,128)S(1)} %get-tuple-element.36), channel_id=1, source_target_pairs={{0,1},{1,2},{2,3},{3,4},{4,5},{5,6},{6,7},{8,9},{9,10},{10,11},{11... | collective-permute-start | bytes 1572872 | tf_op jit(solution)/shard_map/ppermute | solution.py:503
  40.2 3.7 %collective-permute-done.2.refs_3_.refs_5_ = f32[2,4,64,128]{3,2,1,0:T(8,128)S(1)} collective-permute-done((f32[2,4,64,128]{3,2,1,0:T(8,128)S(1)}, f32[2,4,64,128]{3,2,1,0:T(8,128)S(1)}, u32[]{:S(2)}, u32[]{:S(2)}) %collective-permute-start.2) | collective-permute-done | bytes 262176 | tf_op jit(solution)/shard_map/ppermute | solution.py:488
  43.9 1.9 %collective-permute-start.9 = (f32[4,4,64,128]{3,2,1,0:T(8,128)S(1)}, f32[4,4,64,128]{3,2,1,0:T(8,128)S(1)}, u32[]{:S(2)}, u32[]{:S(2)}) collective-permute-start(f32[4,4,64,128]{3,2,1,0:T(8,128)S(1)} %get-tuple-element.32), channel_id=1, source_target_pairs={{1,0},{2,1},{3,2},{4,3},{5,4},{6,5},{7,6},{9,8},{10,9},{11,10},{12... | collective-permute-start | bytes 1572872 | tf_op jit(solution)/shard_map/ppermute | solution.py:508
  45.8 2.6 %collective-permute-done.12.refs_5_ = f32[2,4,64,128]{3,2,1,0:T(8,128)S(1)} collective-permute-done((f32[2,4,64,128]{3,2,1,0:T(8,128)S(1)}, f32[2,4,64,128]{3,2,1,0:T(8,128)S(1)}, u32[]{:S(2)}, u32[]{:S(2)}) %collective-permute-start.12) | collective-permute-done | bytes 262176 | tf_op jit(solution)/shard_map/ppermute | solution.py:488
  48.4 1.5 %collective-permute-start.7 = (f32[2,4,64,128]{3,2,1,0:T(8,128)S(1)}, f32[2,4,64,128]{3,2,1,0:T(8,128)S(1)}, u32[]{:S(2)}, u32[]{:S(2)}) collective-permute-start(f32[2,4,64,128]{3,2,1,0:T(8,128)S(1)} %collective-permute-done.6.refs_1_.refs_7_), channel_id=1, source_target_pairs={{0,16},{8,24},{16,0},{24,8},{1,17},{9,25},{17,1},{25,9},{2,18},{10... | collective-permute-start | bytes 786440 | tf_op jit(solution)/shard_map/ppermute | solution.py:493
  50.4 1.5 %collective-permute-start.17 = (f32[2,4,64,128]{3,2,1,0:T(8,128)S(1)}, f32[2,4,64,128]{3,2,1,0:T(8,128)S(1)}, u32[]{:S(2)}, u32[]{:S(2)}) collective-permute-start(f32[2,4,64,128]{3,2,1,0:T(8,128)S(1)} %collective-permute-done.16.refs_1_.refs_3_.refs_5_), channel_id=1, source_target_pairs={{0,16},{8,24},{16,0},{24,8},{1,17},{9,25},{17,1},{25,9},{2,18},{10... | collective-permute-start | bytes 786440 | tf_op jit(solution)/shard_map/ppermute | solution.py:493
  52.0 5.6 %collective-permute-done.7.refs_7_ = f32[2,4,64,128]{3,2,1,0:T(8,128)S(1)} collective-permute-done((f32[2,4,64,128]{3,2,1,0:T(8,128)S(1)}, f32[2,4,64,128]{3,2,1,0:T(8,128)S(1)}, u32[]{:S(2)}, u32[]{:S(2)}) %collective-permute-start.7) | collective-permute-done | bytes 262176 | tf_op jit(solution)/shard_map/ppermute | solution.py:493
  57.6 1.9 %collective-permute-start.20 = (f32[2,4,64,128]{3,2,1,0:T(8,128)S(1)}, f32[2,4,64,128]{3,2,1,0:T(8,128)S(1)}, u32[]{:S(2)}, u32[]{:S(2)}) collective-permute-start(f32[2,4,64,128]{3,2,1,0:T(8,128)S(1)} %collective-permute-done.7.refs_7_), channel_id=1, source_target_pairs={{0,1},{1,2},{2,3},{3,4},{4,5},{5,6},{6,7},{8,9},{9,10},{10,11},{11... | collective-permute-start | bytes 786440 | tf_op jit(solution)/shard_map/ppermute | solution.py:503
  59.5 3.7 %collective-permute-done.10.refs_3_.refs_1_ = f32[2,4,64,128]{3,2,1,0:T(8,128)S(1)} collective-permute-done((f32[2,4,64,128]{3,2,1,0:T(8,128)S(1)}, f32[2,4,64,128]{3,2,1,0:T(8,128)S(1)}, u32[]{:S(2)}, u32[]{:S(2)}) %collective-permute-start.10) | collective-permute-done | bytes 262176 | tf_op jit(solution)/shard_map/ppermute | solution.py:493
  63.2 1.5 %collective-permute-start.15 = (f32[2,4,64,128]{3,2,1,0:T(8,128)S(1)}, f32[2,4,64,128]{3,2,1,0:T(8,128)S(1)}, u32[]{:S(2)}, u32[]{:S(2)}) collective-permute-start(f32[2,4,64,128]{3,2,1,0:T(8,128)S(1)} %collective-permute-done.14.refs_1_.refs_3_.refs_5_), channel_id=1, source_target_pairs={{0,16},{8,24},{16,0},{24,8},{1,17},{9,25},{17,1},{25,9},{2,18},{10... | collective-permute-start | bytes 786440 | tf_op jit(solution)/shard_map/ppermute | solution.py:493
  64.7 4.1 %collective-permute-done.17.refs_5_.refs_3_.refs_1_ = f32[2,4,64,128]{3,2,1,0:T(8,128)S(1)} collective-permute-done((f32[2,4,64,128]{3,2,1,0:T(8,128)S(1)}, f32[2,4,64,128]{3,2,1,0:T(8,128)S(1)}, u32[]{:S(2)}, u32[]{:S(2)}) %collective-permute-start.17) | collective-permute-done | bytes 262176 | tf_op jit(solution)/shard_map/ppermute | solution.py:493
  72.3 1.9 %collective-permute-start.11 = (f32[2,4,64,128]{3,2,1,0:T(8,128)S(1)}, f32[2,4,64,128]{3,2,1,0:T(8,128)S(1)}, u32[]{:S(2)}, u32[]{:S(2)}) collective-permute-start(f32[2,4,64,128]{3,2,1,0:T(8,128)S(1)} %collective-permute-done.10.refs_3_.refs_1_), channel_id=1, source_target_pairs={{1,0},{2,1},{3,2},{4,3},{5,4},{6,5},{7,6},{9,8},{10,9},{11,10},{12... | collective-permute-start | bytes 786440 | tf_op jit(solution)/shard_map/ppermute | solution.py:508
  74.3 2.1 %shard_map.23 = (f32[2,2,12,64,128]{4,3,2,1,0:T(8,128)S(1)}, f32[2,2,12,64,128]{4,3,2,1,0:T(8,128)S(1)}) custom-call(f32[2,4,64,128]{3,2,1,0:T(8,128)S(1)} %shard_map.19.refs_2_.first.refs_0_.refs_1_, f32[2,4,64,128]{3,2,1,0:T(8,128)S(1)} %get-tuple-element.37.second.refs_1_.refs_0_.refs_2_.refs_3_.refs_4_, ...), custom_call_target="tpu_custom_call" | custom-call | tf_op jit(solution)/shard_map/pallas_call | solution.py:400
  76.3 2.1 %shard_map.20 = (f32[2,2,12,64,128]{4,3,2,1,0:T(8,128)S(1)}, f32[2,2,12,64,128]{4,3,2,1,0:T(8,128)S(1)}) custom-call(f32[2,4,64,128]{3,2,1,0:T(8,128)S(1)} %get-tuple-element.33.refs_0_.refs_3_.refs_2_.refs_4_, f32[2,4,64,128]{3,2,1,0:T(8,128)S(1)} %get-tuple-element.28.refs_1_.refs_0_.refs_2_.refs_4_, ...), custom_call_target="tpu_custom_call" | custom-call | tf_op jit(solution)/shard_map/pallas_call | solution.py:400
  84.8 2.6 %shard_map.21.refs_11_.refs_13_.refs_15_ = f32[2,2,12,64,128]{4,3,2,1,0:T(8,128)S(1)} custom-call(f32[2,4,64,128]{3,2,1,0:T(8,128)S(1)} %get-tuple-element.28.refs_1_.refs_0_.refs_2_.refs_4_, f32[2,4,64,128]{3,2,1,0:T(8,128)S(1)} %collective-permute-done.refs_1_.refs_3_.refs_5_, f32[2,4,64,128]{3,2,1,0:T(8,128)S(1)} %get-tuple-element.29.refs_2_.refs_4_, ...), custom_call_target="tpu_custom_call" | custom-call | tf_op jit(solution)/shard_map/pallas_call | solution.py:446
  93.6 4.1 %shard_map.33 = f32[3,2,32,64,128]{4,3,2,1,0:T(8,128)} custom-call(f32[2,4,64,128]{3,2,1,0:T(8,128)S(1)} %get-tuple-element.28.refs_1_.refs_0_.refs_2_.refs_4_, f32[2,4,64,128]{3,2,1,0:T(8,128)S(1)} %collective-permute-done.1.refs_5_.refs_3_.refs_1_, f32[2,4,64,128]{3,2,1,0:T(8,128)S(1)} %get-tuple-element.29.refs_2_.refs_4_, ...), custom_call_target="tpu_custom_call", output_to_operand_aliasing={{}: (17, {})} | custom-call | tf_op jit(solution)/shard_map/pallas_call | solution.py:468
  (37 shorter events, 29.7 us)
Async XLA Ops:
  1.0 9.2 %collective-permute-start.8 = (f32[2,4,64,128]{3,2,1,0:T(8,128)S(1)}, f32[2,4,64,128]{3,2,1,0:T(8,128)S(1)}, u32[]{:S(2)}, u32[]{:S(2)}) collective-permute-start(f32[2,4,64,128]{3,2,1,0:T(8,128)S(1)} %shard_map.19.refs_2_.first.refs_0_.refs_1_), channel_id=1, source_target_pairs={{0,8},{8,0},{16,24},{24,16},{1,9},{9,1},{17,25},{25,17},{2,10},{10... | collective-permute-start | bytes 786440 | tf_op jit(solution)/shard_map/ppermute | solution.py:488
  3.6 12.2 %collective-permute-start.6 = (f32[2,4,64,128]{3,2,1,0:T(8,128)S(1)}, f32[2,4,64,128]{3,2,1,0:T(8,128)S(1)}, u32[]{:S(2)}, u32[]{:S(2)}) collective-permute-start(f32[2,4,64,128]{3,2,1,0:T(8,128)S(1)} %get-tuple-element.31.refs_0_.refs_4_.fourth.refs_6_), channel_id=1, source_target_pairs={{0,8},{8,0},{16,24},{24,16},{1,9},{9,1},{17,25},{25,17},{2,10},{10... | collective-permute-start | bytes 786440 | tf_op jit(solution)/shard_map/ppermute | solution.py:488
  5.5 16.0 %collective-permute-start.18 = (f32[2,4,64,128]{3,2,1,0:T(8,128)S(1)}, f32[2,4,64,128]{3,2,1,0:T(8,128)S(1)}, u32[]{:S(2)}, u32[]{:S(2)}) collective-permute-start(f32[2,4,64,128]{3,2,1,0:T(8,128)S(1)} %get-tuple-element.37.second.refs_1_.refs_0_.refs_2_.refs_3_.refs_4_), channel_id=1, source_target_pairs={{0,8},{8,0},{16,24},{24,16},{1,9},{9,1},{17,25},{25,17},{2,10},{10... | collective-permute-start | bytes 786440 | tf_op jit(solution)/shard_map/ppermute | solution.py:488
  7.0 20.0 %collective-permute-start.16 = (f32[2,4,64,128]{3,2,1,0:T(8,128)S(1)}, f32[2,4,64,128]{3,2,1,0:T(8,128)S(1)}, u32[]{:S(2)}, u32[]{:S(2)}) collective-permute-start(f32[2,4,64,128]{3,2,1,0:T(8,128)S(1)} %get-tuple-element.40.refs_2_.refs_0_.refs_4_), channel_id=1, source_target_pairs={{0,8},{8,0},{16,24},{24,16},{1,9},{9,1},{17,25},{25,17},{2,10},{10... | collective-permute-start | bytes 786440 | tf_op jit(solution)/shard_map/ppermute | solution.py:488
  7.6 25.1 %collective-permute-start.14 = (f32[2,4,64,128]{3,2,1,0:T(8,128)S(1)}, f32[2,4,64,128]{3,2,1,0:T(8,128)S(1)}, u32[]{:S(2)}, u32[]{:S(2)}) collective-permute-start(f32[2,4,64,128]{3,2,1,0:T(8,128)S(1)} %get-tuple-element.33.refs_0_.refs_3_.refs_2_.refs_4_), channel_id=1, source_target_pairs={{0,8},{8,0},{16,24},{24,16},{1,9},{9,1},{17,25},{25,17},{2,10},{10... | collective-permute-start | bytes 786440 | tf_op jit(solution)/shard_map/ppermute | solution.py:488
  10.2 28.1 %collective-permute-start = (f32[2,4,64,128]{3,2,1,0:T(8,128)S(1)}, f32[2,4,64,128]{3,2,1,0:T(8,128)S(1)}, u32[]{:S(2)}, u32[]{:S(2)}) collective-permute-start(f32[2,4,64,128]{3,2,1,0:T(8,128)S(1)} %get-tuple-element.28.refs_1_.refs_0_.refs_2_.refs_4_), channel_id=1, source_target_pairs={{0,8},{8,0},{16,24},{24,16},{1,9},{9,1},{17,25},{25,17},{2,10},{10... | collective-permute-start | bytes 786440 | tf_op jit(solution)/shard_map/ppermute | solution.py:488
  15.8 28.1 %collective-permute-start.2 = (f32[2,4,64,128]{3,2,1,0:T(8,128)S(1)}, f32[2,4,64,128]{3,2,1,0:T(8,128)S(1)}, u32[]{:S(2)}, u32[]{:S(2)}) collective-permute-start(f32[2,4,64,128]{3,2,1,0:T(8,128)S(1)} %get-tuple-element.29.refs_2_.refs_4_), channel_id=1, source_target_pairs={{0,8},{8,0},{16,24},{24,16},{1,9},{9,1},{17,25},{25,17},{2,10},{10... | collective-permute-start | bytes 786440 | tf_op jit(solution)/shard_map/ppermute | solution.py:488
  21.4 27.0 %collective-permute-start.12 = (f32[2,4,64,128]{3,2,1,0:T(8,128)S(1)}, f32[2,4,64,128]{3,2,1,0:T(8,128)S(1)}, u32[]{:S(2)}, u32[]{:S(2)}) collective-permute-start(f32[2,4,64,128]{3,2,1,0:T(8,128)S(1)} %get-tuple-element.30.refs_3_.third.refs_4_), channel_id=1, source_target_pairs={{0,8},{8,0},{16,24},{24,16},{1,9},{9,1},{17,25},{25,17},{2,10},{10... | collective-permute-start | bytes 786440 | tf_op jit(solution)/shard_map/ppermute | solution.py:488
  27.1 22.9 %collective-permute-start.4 = (f32[2,4,64,128]{3,2,1,0:T(8,128)S(1)}, f32[2,4,64,128]{3,2,1,0:T(8,128)S(1)}, u32[]{:S(2)}, u32[]{:S(2)}) collective-permute-start(f32[2,4,64,128]{3,2,1,0:T(8,128)S(1)} %get-tuple-element.30.refs_3_.third.refs_4_), channel_id=1, source_target_pairs={{0,16},{8,24},{16,0},{24,8},{1,17},{9,25},{17,1},{25,9},{2,18},{10... | collective-permute-start | bytes 786440 | tf_op jit(solution)/shard_map/ppermute | solution.py:498
  32.7 17.8 %collective-permute-start.19 = (f32[2,4,64,128]{3,2,1,0:T(8,128)S(1)}, f32[2,4,64,128]{3,2,1,0:T(8,128)S(1)}, u32[]{:S(2)}, u32[]{:S(2)}) collective-permute-start(f32[2,4,64,128]{3,2,1,0:T(8,128)S(1)} %collective-permute-done.18.refs_1_.refs_3_.refs_4_), channel_id=1, source_target_pairs={{0,16},{8,24},{16,0},{24,8},{1,17},{9,25},{17,1},{25,9},{2,18},{10... | collective-permute-start | bytes 786440 | tf_op jit(solution)/shard_map/ppermute | solution.py:493
  38.3 32.0 %collective-permute-start.13 = (f32[4,4,64,128]{3,2,1,0:T(8,128)S(1)}, f32[4,4,64,128]{3,2,1,0:T(8,128)S(1)}, u32[]{:S(2)}, u32[]{:S(2)}) collective-permute-start(f32[4,4,64,128]{3,2,1,0:T(8,128)S(1)} %get-tuple-element.36), channel_id=1, source_target_pairs={{0,1},{1,2},{2,3},{3,4},{4,5},{5,6},{6,7},{8,9},{9,10},{10,11},{11... | collective-permute-start | bytes 1572872 | tf_op jit(solution)/shard_map/ppermute | solution.py:503
  43.9 26.9 %collective-permute-start.9 = (f32[4,4,64,128]{3,2,1,0:T(8,128)S(1)}, f32[4,4,64,128]{3,2,1,0:T(8,128)S(1)}, u32[]{:S(2)}, u32[]{:S(2)}) collective-permute-start(f32[4,4,64,128]{3,2,1,0:T(8,128)S(1)} %get-tuple-element.32), channel_id=1, source_target_pairs={{1,0},{2,1},{3,2},{4,3},{5,4},{6,5},{7,6},{9,8},{10,9},{11,10},{12... | collective-permute-start | bytes 1572872 | tf_op jit(solution)/shard_map/ppermute | solution.py:508
  48.4 9.2 %collective-permute-start.7 = (f32[2,4,64,128]{3,2,1,0:T(8,128)S(1)}, f32[2,4,64,128]{3,2,1,0:T(8,128)S(1)}, u32[]{:S(2)}, u32[]{:S(2)}) collective-permute-start(f32[2,4,64,128]{3,2,1,0:T(8,128)S(1)} %collective-permute-done.6.refs_1_.refs_7_), channel_id=1, source_target_pairs={{0,16},{8,24},{16,0},{24,8},{1,17},{9,25},{17,1},{25,9},{2,18},{10... | collective-permute-start | bytes 786440 | tf_op jit(solution)/shard_map/ppermute | solution.py:493
  49.9 13.3 %collective-permute-start.10 = (f32[2,4,64,128]{3,2,1,0:T(8,128)S(1)}, f32[2,4,64,128]{3,2,1,0:T(8,128)S(1)}, u32[]{:S(2)}, u32[]{:S(2)}) collective-permute-start(f32[2,4,64,128]{3,2,1,0:T(8,128)S(1)} %collective-permute-done.8.refs_3_.refs_1_.refs_2_), channel_id=1, source_target_pairs={{0,16},{8,24},{16,0},{24,8},{1,17},{9,25},{17,1},{25,9},{2,18},{10... | collective-permute-start | bytes 786440 | tf_op jit(solution)/shard_map/ppermute | solution.py:493
  50.4 18.4 %collective-permute-start.17 = (f32[2,4,64,128]{3,2,1,0:T(8,128)S(1)}, f32[2,4,64,128]{3,2,1,0:T(8,128)S(1)}, u32[]{:S(2)}, u32[]{:S(2)}) collective-permute-start(f32[2,4,64,128]{3,2,1,0:T(8,128)S(1)} %collective-permute-done.16.refs_1_.refs_3_.refs_5_), channel_id=1, source_target_pairs={{0,16},{8,24},{16,0},{24,8},{1,17},{9,25},{17,1},{25,9},{2,18},{10... | collective-permute-start | bytes 786440 | tf_op jit(solution)/shard_map/ppermute | solution.py:493
  57.6 14.8 %collective-permute-start.20 = (f32[2,4,64,128]{3,2,1,0:T(8,128)S(1)}, f32[2,4,64,128]{3,2,1,0:T(8,128)S(1)}, u32[]{:S(2)}, u32[]{:S(2)}) collective-permute-start(f32[2,4,64,128]{3,2,1,0:T(8,128)S(1)} %collective-permute-done.7.refs_7_), channel_id=1, source_target_pairs={{0,1},{1,2},{2,3},{3,4},{4,5},{5,6},{6,7},{8,9},{9,10},{10,11},{11... | collective-permute-start | bytes 786440 | tf_op jit(solution)/shard_map/ppermute | solution.py:503
  63.2 26.6 %collective-permute-start.15 = (f32[2,4,64,128]{3,2,1,0:T(8,128)S(1)}, f32[2,4,64,128]{3,2,1,0:T(8,128)S(1)}, u32[]{:S(2)}, u32[]{:S(2)}) collective-permute-start(f32[2,4,64,128]{3,2,1,0:T(8,128)S(1)} %collective-permute-done.14.refs_1_.refs_3_.refs_5_), channel_id=1, source_target_pairs={{0,16},{8,24},{16,0},{24,8},{1,17},{9,25},{17,1},{25,9},{2,18},{10... | collective-permute-start | bytes 786440 | tf_op jit(solution)/shard_map/ppermute | solution.py:493
  68.8 22.2 %collective-permute-start.1 = (f32[2,4,64,128]{3,2,1,0:T(8,128)S(1)}, f32[2,4,64,128]{3,2,1,0:T(8,128)S(1)}, u32[]{:S(2)}, u32[]{:S(2)}) collective-permute-start(f32[2,4,64,128]{3,2,1,0:T(8,128)S(1)} %collective-permute-done.refs_1_.refs_3_.refs_5_), channel_id=1, source_target_pairs={{0,16},{8,24},{16,0},{24,8},{1,17},{9,25},{17,1},{25,9},{2,18},{10... | collective-permute-start | bytes 786440 | tf_op jit(solution)/shard_map/ppermute | solution.py:493
  70.3 21.9 %collective-permute-start.3 = (f32[2,4,64,128]{3,2,1,0:T(8,128)S(1)}, f32[2,4,64,128]{3,2,1,0:T(8,128)S(1)}, u32[]{:S(2)}, u32[]{:S(2)}) collective-permute-start(f32[2,4,64,128]{3,2,1,0:T(8,128)S(1)} %collective-permute-done.2.refs_3_.refs_5_), channel_id=1, source_target_pairs={{0,16},{8,24},{16,0},{24,8},{1,17},{9,25},{17,1},{25,9},{2,18},{10... | collective-permute-start | bytes 786440 | tf_op jit(solution)/shard_map/ppermute | solution.py:493
  70.8 22.8 %collective-permute-start.5 = (f32[2,4,64,128]{3,2,1,0:T(8,128)S(1)}, f32[2,4,64,128]{3,2,1,0:T(8,128)S(1)}, u32[]{:S(2)}, u32[]{:S(2)}) collective-permute-start(f32[2,4,64,128]{3,2,1,0:T(8,128)S(1)} %collective-permute-done.4), channel_id=1, source_target_pairs={{0,8},{8,0},{16,24},{24,16},{1,9},{9,1},{17,25},{25,17},{2,10},{10... | collective-permute-start | bytes 786440 | tf_op jit(solution)/shard_map/ppermute | solution.py:488
  72.3 21.3 %collective-permute-start.11 = (f32[2,4,64,128]{3,2,1,0:T(8,128)S(1)}, f32[2,4,64,128]{3,2,1,0:T(8,128)S(1)}, u32[]{:S(2)}, u32[]{:S(2)}) collective-permute-start(f32[2,4,64,128]{3,2,1,0:T(8,128)S(1)} %collective-permute-done.10.refs_3_.refs_1_), channel_id=1, source_target_pairs={{1,0},{2,1},{3,2},{4,3},{5,4},{6,5},{7,6},{9,8},{10,9},{11,10},{12... | collective-permute-start | bytes 786440 | tf_op jit(solution)/shard_map/ppermute | solution.py:508

commit v2 on v1

--- a/solution.py
+++ b/solution.py
@@ -232,14 +232,14 @@
         done(i)
 
 
-def readers(j, count, rims, refs):
+def readers(j, count, side, refs):
     depth = BLOCK * count
     own = [(ref, 0, BLOCK * k[1], BLOCK) for k, ref in refs.items() if k[0] == "own"]
     theirs = [(ref, 0, BLOCK * k[1], BLOCK) for k, ref in refs.items() if k[0] == "side"]
     for name, first in (("low", -BLOCK), ("high", depth)):
         if (name,) in refs:
             own.append((refs[name,], 0, first, BLOCK))
-            theirs.append((refs[name + rims[0],], rims[1], first, BLOCK))
+            theirs.append((refs[name,], 2 * side, first, BLOCK))
     base = BLOCK * (j - 1)
     return plane_of(own, base), plane_of(theirs, base)
 
@@ -253,7 +253,7 @@
     near = lax.rem(lax.axis_index("phase"), 2)
     rows, width = refs["own", js[0]].shape[2:]
     clear_rims(tz, rows)
-    own, theirs = readers(js[0], count, ("", 2), refs)
+    own, theirs = readers(js[0], count, 1, refs)
 
     def tables(i):
         j, z = js[i // BLOCK], bases[i // BLOCK] + i % BLOCK
@@ -295,7 +295,7 @@
         padded[a, 0:8, :] = zero
         padded[a, rows + 8 : rows + 16, :] = zero
     lane = lax.broadcasted_iota(jnp.int32, (8, width), 1)
-    own, theirs = readers(js[0], count, ("_b", 0), refs)
+    own, theirs = readers(js[0], count, 2, refs)
 
     def tables(i):
         j = js[i // BLOCK]
@@ -373,24 +373,59 @@
     return dict(zip(bs, outs))
 
 
+def copied(source, target):
+    for k in range(source.shape[0]):
+        target[k] = source[k]
+
+
 def pack_kernel(*refs):
-    for n in range(2):
-        for k in range(2):
+    ends, tops, (inner, outer) = refs[:3], refs[3:6], refs[6:]
+    even = lax.rem(lax.axis_index("slab"), 2) == 0
+
+    def fill(target, parts):
+        for k, part in enumerate(parts):
             for a in range(2):
-                refs[4 + n][2 * k + a] = refs[2 * n + k][a]
-
-
-def packed(groups):
-    shape = groups[0][0].shape
-    out = like(2 * shape[0], *shape[1:])
+                target[2 * k + a] = part[a]
+
+    @pl.when(even)
+    def _():
+        fill(inner, ends)
+        fill(outer, tops)
+
+    @pl.when(jnp.logical_not(even))
+    def _():
+        fill(inner, tops)
+        fill(outer, ends)
+
+
+def unpack_kernel(inner, outer, low, high):
+    even = lax.rem(lax.axis_index("slab"), 2) == 0
+
+    @pl.when(even)
+    def _():
+        copied(outer, low)
+        copied(inner, high)
+
+    @pl.when(jnp.logical_not(even))
+    def _():
+        copied(inner, low)
+        copied(outer, high)
+
+
+def sorted_pair(kernel, operands, out):
     return pl.pallas_call(
-        pack_kernel,
-        out_shape=(out, out),
-        in_specs=[VMEM] * 4,
-        out_specs=(VMEM, VMEM),
-        compiler_params=params(6),
-        name="pack",
-    )(*groups[0], *groups[1])
+        kernel, out_shape=(out, out), in_specs=[VMEM] * len(operands), out_specs=(VMEM, VMEM), compiler_params=params(6)
+    )(*operands)
+
+
+def swapped_rims(ends, tops):
+    out = like(3 * ends[0].shape[0], *ends[0].shape[1:])
+    n = lax.axis_size("slab")
+    inner, outer = sorted_pair(pack_kernel, (*ends, *tops), out)
+    pairs = [(q, q + 1) for q in range(1, n - 1, 2)] + [(q + 1, q) for q in range(1, n - 1, 2)]
+    outer = lax.ppermute(outer, "slab", pairs)
+    inner = lax.ppermute(inner, "slab", [(q, q ^ 1) for q in range(n)])
+    return sorted_pair(unpack_kernel, (inner, outer), out)
 
 
 def own_inner(low, high, blocks):
@@ -421,16 +456,16 @@
     )(low, high, *blocks)
 
 
-def gather_operands(js, count, own, side, rims):
+def gather_operands(js, count, own, side, low, high):
     wanted = {}
     for b in range(js[0] - 1, js[-1] + 2):
         if 0 <= b < count:
             wanted["own", b] = own[b]
             wanted["side", b] = side[b]
+        elif b < 0:
+            wanted["low",] = low
         else:
-            for name in rims:
-                if name.startswith("low" if b < 0 else "high"):
-                    wanted[name,] = rims[name]
+            wanted["high",] = high
     return wanted
 
 
@@ -438,9 +473,9 @@
     return [ANY if k == ("forces",) else VMEM for k in wanted]
 
 
-def first_side(js, count, own, side, rims, stats, accs, bases):
+def first_side(js, count, own, side, low, high, stats, accs, bases):
     rows, width = own[0].shape[2:]
-    wanted = gather_operands(js, count, own, side, rims)
+    wanted = gather_operands(js, count, own, side, low, high)
     for j in js:
         wanted["stats", j], wanted["acc", j] = stats[j], accs[j]
     return pl.pallas_call(
@@ -453,9 +488,9 @@
     )(*wanted.values())
 
 
-def last_side(js, count, own, side, rims, stats, bases, sums, before, block, forces, final):
+def last_side(js, count, own, side, low, high, stats, bases, sums, before, block, forces, final):
     rows, width = own[0].shape[2:]
-    wanted = gather_operands(js, count, own, side, rims)
+    wanted = gather_operands(js, count, own, side, low, high)
     for j in js:
         wanted["stats", j], wanted["acc", j] = stats[j], sums[j][0]
     if before is not None:
@@ -498,20 +533,10 @@
     return lax.ppermute(value, "phase", [(q, (q + (n - 2 if q % 2 == 0 else 2)) % n) for q in range(n)])
 
 
-def upward(value):
-    n = lax.axis_size("slab")
-    return lax.ppermute(value, "slab", [(q, q + 1) for q in range(n - 1)])
-
-
-def downward(value):
-    n = lax.axis_size("slab")
-    return lax.ppermute(value, "slab", [(q + 1, q) for q in range(n - 1)])
-
-
 def local_forces(images):
     count = images.shape[1] // BLOCK
     assert images.shape[0] == 2 and images.shape[1] == BLOCK * count and count >= 6
-    assert lax.axis_size("phase") % 2 == 0
+    assert lax.axis_size("phase") % 2 == 0 and lax.axis_size("slab") % 2 == 0
     half = (count + 1) // 2
 
     top, end, turned = 0, count - 1, count - 2
@@ -521,12 +546,11 @@
     one = {b: across(blocks[b]) for b in blocks}
     two = {b: onward(one[b]) for b in blocks if b != turned}
     two[turned] = across(yonder(blocks[turned]))
-    low, high = packed([(blocks[end], one[end]), (blocks[top], one[top])])
-    rims = {"low": upward(low), "high": downward(high), "low_b": upward(two[end]), "high_b": downward(two[top])}
+    low, high = swapped_rims((blocks[end], one[end], two[end]), (blocks[top], one[top], two[top]))
 
     near_half = own_inner(1, half, blocks)
     far_half = own_inner(half, count - 1, blocks)
-    outer = own_ends(rims["low"], rims["high"], blocks[0], blocks[1], blocks[end - 1], blocks[end])
+    outer = own_ends(low, high, blocks[0], blocks[1], blocks[end - 1], blocks[end])
     stats, acc, base = {}, {}, {}
     for j in range(count):
         if j in (0, count - 1):
@@ -535,16 +559,15 @@
             (stats[j], acc[j]), base[j] = near_half, BLOCK * (j - 1)
         else:
             (stats[j], acc[j]), base[j] = far_half, BLOCK * (j - half)
-    shared = {name: rims[name] for name in ("low", "high")}
     sums = {}
     for js in first_groups(count):
-        total = first_side(js, count, blocks, one, shared, stats, acc, base)
+        total = first_side(js, count, blocks, one, low, high, stats, acc, base)
         sums.update({j: (total, BLOCK * k) for k, j in enumerate(js)})
     forces, block, before = None, None, None
     groups = last_groups(count)
     for js in groups:
         forces, block = last_side(
-            js, count, blocks, two, rims, stats, base, sums, before, block, forces, js == groups[-1]
+            js, count, blocks, two, low, high, stats, base, sums, before, block, forces, js == groups[-1]
         )
         before = js[0]
     return forces
@@ -555,7 +578,7 @@
 
 
 def last_groups(count):
-    return [(j,) for j in range(count - 3)] + [tuple(range(count - 3, count))]
+    return [(j,) for j in (1, 2, 0, *range(3, count - 3))] + [tuple(range(count - 3, count))]
 
 
 def solution(mesh):

time: 99.6 us -> 91.2 us (0.916)
  starting transfers between devices: 29.5 us -> 21.3 us
    ppermute x4 -> x2, starting transfers between devices: 7.64 us -> 2.52 us  [the longest x1 2.45 us: swapped_rims(): outer = lax.ppermute(outer, 'slab', pairs)]
    ppermute x7, starting transfers between devices: 8.61 us -> 6.58 us  [onward(): lax.ppermute(value, 'phase', [(q, (q + (2 if q % 2 == 0 else n - 2)) % n)...]
    ppermute x1, starting transfers between devices: 1.52 us -> 0.51 us  [yonder(): lax.ppermute(value, 'phase', [(q, (q + (n - 2 if q % 2 == 0 else 2)) % n)...]
  transfers between devices with their start and end apart: 21 -> 19, of which waited for: 11 -> 11; matrix products, arithmetic and copies ran while one was open for 0% -> 0% of each run, Pallas kernels for 22% -> 24%
where the time goes in v2:
time: 91.2 us; the launch traced here: 89.5 us
  waiting for transfers between devices  41 us (45%)
  Pallas kernels  26.8 us (29%)
  starting transfers between devices  21.3 us (23%)
    ppermute x9, waiting for transfers between devices, across(): return lax.ppermute(value, 'phase', [(q, q ^ 1) for q in range(n)])  27.1 us
    ppermute x7, waiting for transfers between devices, onward(): lax.ppermute(value, 'phase', [(q, (q + (2 if q % 2 == 0 else n - 2)) % n)...  13.9 us
    ppermute x9, starting transfers between devices, across(): return lax.ppermute(value, 'phase', [(q, q ^ 1) for q in range(n)])  11.7 us
    pallas_call x6, Pallas kernels, last_side(): pl.pallas_call(functools.partial(last_kernel, js, count, [bases[j] for j...  10 us
    pallas_call x6, Pallas kernels, first_side(): pl.pallas_call(functools.partial(first_kernel, js, count, [bases[j] for j...  7.55 us
    ppermute x7, starting transfers between devices, onward(): lax.ppermute(value, 'phase', [(q, (q + (2 if q % 2 == 0 else n - 2)) % n)...  6.58 us
    pallas_call x2, Pallas kernels, own_inner(): pl.pallas_call(functools.partial(own_inner_kernel, size), out_shape=(shap...  4.1 us
    pallas_call x3, Pallas kernels, cut_blocks(): pl.pallas_call(functools.partial(cut_kernel, bs), out_shape=[like(phases,...  3.31 us
  transfers between devices with their start and end apart: 19, of which 11 were waited for; matrix products, arithmetic and copies ran while one was open for 0% of the time, Pallas kernels for 24%

profile of v2, /device:TPU:16, one launch (start us, length us, event | category | flops | bytes accessed | tf_op | source)
XLA Modules:
  0.0 89.5 jit_solution(4175147138734474775)
XLA Ops:
  1.0 1.6 %collective-permute-start.8 = (f32[2,4,64,128]{3,2,1,0:T(8,128)S(1)}, f32[2,4,64,128]{3,2,1,0:T(8,128)S(1)}, u32[]{:S(2)}, u32[]{:S(2)}) collective-permute-start(f32[2,4,64,128]{3,2,1,0:T(8,128)S(1)} %shard_map.19.refs_3_.first.refs_0_.refs_1_), channel_id=1, source_target_pairs={{0,8},{8,0},{16,24},{24,16},{1,9},{9,1},{17,25},{25,17},{2,10},{10... | collective-permute-start | bytes 786440 | tf_op jit(solution)/shard_map/ppermute | solution.py:523
  4.2 6.0 %collective-permute-done.8.refs_4_.refs_2_.refs_1_ = f32[2,4,64,128]{3,2,1,0:T(8,128)S(1)} collective-permute-done((f32[2,4,64,128]{3,2,1,0:T(8,128)S(1)}, f32[2,4,64,128]{3,2,1,0:T(8,128)S(1)}, u32[]{:S(2)}, u32[]{:S(2)}) %collective-permute-start.8) | collective-permute-done | bytes 262176 | tf_op jit(solution)/shard_map/ppermute | solution.py:523
  10.2 1.5 %collective-permute-start.9 = (f32[2,4,64,128]{3,2,1,0:T(8,128)S(1)}, f32[2,4,64,128]{3,2,1,0:T(8,128)S(1)}, u32[]{:S(2)}, u32[]{:S(2)}) collective-permute-start(f32[2,4,64,128]{3,2,1,0:T(8,128)S(1)} %collective-permute-done.8.refs_4_.refs_2_.refs_1_), channel_id=1, source_target_pairs={{0,16},{8,24},{16,0},{24,8},{1,17},{9,25},{17,1},{25,9},{2,18},{10... | collective-permute-start | bytes 786440 | tf_op jit(solution)/shard_map/ppermute | solution.py:528
  11.7 3.0 %collective-permute-done.6.refs_1_.refs_7_ = f32[2,4,64,128]{3,2,1,0:T(8,128)S(1)} collective-permute-done((f32[2,4,64,128]{3,2,1,0:T(8,128)S(1)}, f32[2,4,64,128]{3,2,1,0:T(8,128)S(1)}, u32[]{:S(2)}, u32[]{:S(2)}) %collective-permute-start.6) | collective-permute-done | bytes 262176 | tf_op jit(solution)/shard_map/ppermute | solution.py:523
  14.7 1.5 %collective-permute-start.7 = (f32[2,4,64,128]{3,2,1,0:T(8,128)S(1)}, f32[2,4,64,128]{3,2,1,0:T(8,128)S(1)}, u32[]{:S(2)}, u32[]{:S(2)}) collective-permute-start(f32[2,4,64,128]{3,2,1,0:T(8,128)S(1)} %collective-permute-done.6.refs_1_.refs_7_), channel_id=1, source_target_pairs={{0,16},{8,24},{16,0},{24,8},{1,17},{9,25},{17,1},{25,9},{2,18},{10... | collective-permute-start | bytes 786440 | tf_op jit(solution)/shard_map/ppermute | solution.py:528
  17.5 1.6 %collective-permute-start.17 = (f32[2,4,64,128]{3,2,1,0:T(8,128)S(1)}, f32[2,4,64,128]{3,2,1,0:T(8,128)S(1)}, u32[]{:S(2)}, u32[]{:S(2)}) collective-permute-start(f32[2,4,64,128]{3,2,1,0:T(8,128)S(1)} %get-tuple-element.41.second.refs_1_.refs_3_.refs_0_.refs_2_), channel_id=1, source_target_pairs={{0,8},{8,0},{16,24},{24,16},{1,9},{9,1},{17,25},{25,17},{2,10},{10... | collective-permute-start | bytes 786440 | tf_op jit(solution)/shard_map/ppermute | solution.py:523
  19.6 1.5 %collective-permute-start.13 = (f32[2,4,64,128]{3,2,1,0:T(8,128)S(1)}, f32[2,4,64,128]{3,2,1,0:T(8,128)S(1)}, u32[]{:S(2)}, u32[]{:S(2)}) collective-permute-start(f32[2,4,64,128]{3,2,1,0:T(8,128)S(1)} %get-tuple-element.37.refs_0_.refs_3_.refs_2_.refs_4_), channel_id=1, source_target_pairs={{0,8},{8,0},{16,24},{24,16},{1,9},{9,1},{17,25},{25,17},{2,10},{10... | collective-permute-start | bytes 786440 | tf_op jit(solution)/shard_map/ppermute | solution.py:523
  22.4 2.4 %collective-permute-start.11 = (f32[6,4,64,128]{3,2,1,0:T(8,128)S(1)}, f32[6,4,64,128]{3,2,1,0:T(8,128)S(1)}, u32[]{:S(2)}, u32[]{:S(2)}) collective-permute-start(f32[6,4,64,128]{3,2,1,0:T(8,128)S(1)} %get-tuple-element.35), channel_id=1, source_target_pairs={{1,2},{3,4},{5,6},{2,1},{4,3},{6,5},{9,10},{11,12},{13,14},{10,9},... | collective-permute-start | bytes 2359304 | tf_op jit(solution)/shard_map/ppermute | solution.py:426
  24.8 1.9 %collective-permute-done.17.refs_4_.refs_1_.refs_3_ = f32[2,4,64,128]{3,2,1,0:T(8,128)S(1)} collective-permute-done((f32[2,4,64,128]{3,2,1,0:T(8,128)S(1)}, f32[2,4,64,128]{3,2,1,0:T(8,128)S(1)}, u32[]{:S(2)}, u32[]{:S(2)}) %collective-permute-start.17) | collective-permute-done | bytes 262176 | tf_op jit(solution)/shard_map/ppermute | solution.py:523
  26.8 1.5 %collective-permute-start = (f32[2,4,64,128]{3,2,1,0:T(8,128)S(1)}, f32[2,4,64,128]{3,2,1,0:T(8,128)S(1)}, u32[]{:S(2)}, u32[]{:S(2)}) collective-permute-start(f32[2,4,64,128]{3,2,1,0:T(8,128)S(1)} %get-tuple-element.30.refs_1_.refs_0_.refs_2_.refs_4_), channel_id=1, source_target_pairs={{0,8},{8,0},{16,24},{24,16},{1,9},{9,1},{17,25},{25,17},{2,10},{10... | collective-permute-start | bytes 786440 | tf_op jit(solution)/shard_map/ppermute | solution.py:523
  28.3 4.1 %collective-permute-done.15.refs_1_.refs_3_.refs_5_ = f32[2,4,64,128]{3,2,1,0:T(8,128)S(1)} collective-permute-done((f32[2,4,64,128]{3,2,1,0:T(8,128)S(1)}, f32[2,4,64,128]{3,2,1,0:T(8,128)S(1)}, u32[]{:S(2)}, u32[]{:S(2)}) %collective-permute-start.15) | collective-permute-done | bytes 262176 | tf_op jit(solution)/shard_map/ppermute | solution.py:523
  33.9 4.1 %collective-permute-done.13.refs_1_.refs_3_.refs_5_ = f32[2,4,64,128]{3,2,1,0:T(8,128)S(1)} collective-permute-done((f32[2,4,64,128]{3,2,1,0:T(8,128)S(1)}, f32[2,4,64,128]{3,2,1,0:T(8,128)S(1)}, u32[]{:S(2)}, u32[]{:S(2)}) %collective-permute-start.13) | collective-permute-done | bytes 262176 | tf_op jit(solution)/shard_map/ppermute | solution.py:523
  38.5 5.1 %collective-permute-done.refs_1_.refs_3_.refs_5_ = f32[2,4,64,128]{3,2,1,0:T(8,128)S(1)} collective-permute-done((f32[2,4,64,128]{3,2,1,0:T(8,128)S(1)}, f32[2,4,64,128]{3,2,1,0:T(8,128)S(1)}, u32[]{:S(2)}, u32[]{:S(2)}) %collective-permute-start) | collective-permute-done | bytes 262176 | tf_op jit(solution)/shard_map/ppermute | solution.py:523
  44.1 2.8 %collective-permute-done.2.refs_3_.refs_5_ = f32[2,4,64,128]{3,2,1,0:T(8,128)S(1)} collective-permute-done((f32[2,4,64,128]{3,2,1,0:T(8,128)S(1)}, f32[2,4,64,128]{3,2,1,0:T(8,128)S(1)}, u32[]{:S(2)}, u32[]{:S(2)}) %collective-permute-start.2) | collective-permute-done | bytes 262176 | tf_op jit(solution)/shard_map/ppermute | solution.py:523
  47.5 1.5 %collective-permute-start.14 = (f32[2,4,64,128]{3,2,1,0:T(8,128)S(1)}, f32[2,4,64,128]{3,2,1,0:T(8,128)S(1)}, u32[]{:S(2)}, u32[]{:S(2)}) collective-permute-start(f32[2,4,64,128]{3,2,1,0:T(8,128)S(1)} %collective-permute-done.13.refs_1_.refs_3_.refs_5_), channel_id=1, source_target_pairs={{0,16},{8,24},{16,0},{24,8},{1,17},{9,25},{17,1},{25,9},{2,18},{10... | collective-permute-start | bytes 786440 | tf_op jit(solution)/shard_map/ppermute | solution.py:528
  49.0 3.6 %collective-permute-done.18.refs_3_.refs_1_.refs_4_ = f32[2,4,64,128]{3,2,1,0:T(8,128)S(1)} collective-permute-done((f32[2,4,64,128]{3,2,1,0:T(8,128)S(1)}, f32[2,4,64,128]{3,2,1,0:T(8,128)S(1)}, u32[]{:S(2)}, u32[]{:S(2)}) %collective-permute-start.18) | collective-permute-done | bytes 262176 | tf_op jit(solution)/shard_map/ppermute | solution.py:528
  52.6 1.5 %collective-permute-start.12 = (f32[2,4,64,128]{3,2,1,0:T(8,128)S(1)}, f32[2,4,64,128]{3,2,1,0:T(8,128)S(1)}, u32[]{:S(2)}, u32[]{:S(2)}) collective-permute-start(f32[2,4,64,128]{3,2,1,0:T(8,128)S(1)} %get-tuple-element.32.refs_3_.third.refs_4_), channel_id=1, source_target_pairs={{0,8},{8,0},{16,24},{24,16},{1,9},{9,1},{17,25},{25,17},{2,10},{10... | collective-permute-start | bytes 786440 | tf_op jit(solution)/shard_map/ppermute | solution.py:523
  54.1 4.1 %collective-permute-done.16.refs_5_.refs_3_.refs_1_ = f32[2,4,64,128]{3,2,1,0:T(8,128)S(1)} collective-permute-done((f32[2,4,64,128]{3,2,1,0:T(8,128)S(1)}, f32[2,4,64,128]{3,2,1,0:T(8,128)S(1)}, u32[]{:S(2)}, u32[]{:S(2)}) %collective-permute-start.16) | collective-permute-done | bytes 262176 | tf_op jit(solution)/shard_map/ppermute | solution.py:528
  58.7 5.1 %collective-permute-done.14.refs_5_.refs_3_.refs_1_ = f32[2,4,64,128]{3,2,1,0:T(8,128)S(1)} collective-permute-done((f32[2,4,64,128]{3,2,1,0:T(8,128)S(1)}, f32[2,4,64,128]{3,2,1,0:T(8,128)S(1)}, u32[]{:S(2)}, u32[]{:S(2)}) %collective-permute-start.14) | collective-permute-done | bytes 262176 | tf_op jit(solution)/shard_map/ppermute | solution.py:528
  64.3 1.5 %collective-permute-start.5 = (f32[2,4,64,128]{3,2,1,0:T(8,128)S(1)}, f32[2,4,64,128]{3,2,1,0:T(8,128)S(1)}, u32[]{:S(2)}, u32[]{:S(2)}) collective-permute-start(f32[2,4,64,128]{3,2,1,0:T(8,128)S(1)} %collective-permute-done.4), channel_id=1, source_target_pairs={{0,8},{8,0},{16,24},{24,16},{1,9},{9,1},{17,25},{25,17},{2,10},{10... | collective-permute-start | bytes 786440 | tf_op jit(solution)/shard_map/ppermute | solution.py:523
  65.8 2.0 %shard_map.25 = (f32[2,2,12,64,128]{4,3,2,1,0:T(8,128)S(1)}, f32[2,2,12,64,128]{4,3,2,1,0:T(8,128)S(1)}) custom-call(f32[2,4,64,128]{3,2,1,0:T(8,128)S(1)} %shard_map.19.refs_3_.first.refs_0_.refs_1_, f32[2,4,64,128]{3,2,1,0:T(8,128)S(1)} %get-tuple-element.41.second.refs_1_.refs_3_.refs_0_.refs_2_, ...), custom_call_target="tpu_custom_call" | custom-call | tf_op jit(solution)/shard_map/pallas_call | solution.py:435
  67.9 2.1 %shard_map.22 = (f32[2,2,12,64,128]{4,3,2,1,0:T(8,128)S(1)}, f32[2,2,12,64,128]{4,3,2,1,0:T(8,128)S(1)}) custom-call(f32[2,4,64,128]{3,2,1,0:T(8,128)S(1)} %get-tuple-element.37.refs_0_.refs_3_.refs_2_.refs_4_, f32[2,4,64,128]{3,2,1,0:T(8,128)S(1)} %get-tuple-element.30.refs_1_.refs_0_.refs_2_.refs_4_, ...), custom_call_target="tpu_custom_call" | custom-call | tf_op jit(solution)/shard_map/pallas_call | solution.py:435
  79.1 2.6 %shard_map.23.refs_10_.refs_12_.refs_14_ = f32[2,2,12,64,128]{4,3,2,1,0:T(8,128)S(1)} custom-call(f32[2,4,64,128]{3,2,1,0:T(8,128)S(1)} %get-tuple-element.30.refs_1_.refs_0_.refs_2_.refs_4_, f32[2,4,64,128]{3,2,1,0:T(8,128)S(1)} %collective-permute-done.refs_1_.refs_3_.refs_5_, f32[2,4,64,128]{3,2,1,0:T(8,128)S(1)} %get-tuple-element.31.refs_2_.refs_4_, ...), custom_call_target="tpu_custom_call" | custom-call | tf_op jit(solution)/shard_map/pallas_call | solution.py:481
  85.3 4.1 %shard_map.35 = f32[3,2,32,64,128]{4,3,2,1,0:T(8,128)} custom-call(f32[2,4,64,128]{3,2,1,0:T(8,128)S(1)} %get-tuple-element.30.refs_1_.refs_0_.refs_2_.refs_4_, f32[2,4,64,128]{3,2,1,0:T(8,128)S(1)} %collective-permute-done.1.refs_5_.refs_3_.refs_1_, f32[2,4,64,128]{3,2,1,0:T(8,128)S(1)} %get-tuple-element.31.refs_2_.refs_4_, ...), custom_call_target="tpu_custom_call", output_to_operand_aliasing={{}: (16, {})} | custom-call | tf_op jit(solution)/shard_map/pallas_call | solution.py:503
  (34 shorter events, 22.4 us)
Async XLA Ops:
  1.0 9.2 %collective-permute-start.8 = (f32[2,4,64,128]{3,2,1,0:T(8,128)S(1)}, f32[2,4,64,128]{3,2,1,0:T(8,128)S(1)}, u32[]{:S(2)}, u32[]{:S(2)}) collective-permute-start(f32[2,4,64,128]{3,2,1,0:T(8,128)S(1)} %shard_map.19.refs_3_.first.refs_0_.refs_1_), channel_id=1, source_target_pairs={{0,8},{8,0},{16,24},{24,16},{1,9},{9,1},{17,25},{25,17},{2,10},{10... | collective-permute-start | bytes 786440 | tf_op jit(solution)/shard_map/ppermute | solution.py:523
  3.6 11.1 %collective-permute-start.6 = (f32[2,4,64,128]{3,2,1,0:T(8,128)S(1)}, f32[2,4,64,128]{3,2,1,0:T(8,128)S(1)}, u32[]{:S(2)}, u32[]{:S(2)}) collective-permute-start(f32[2,4,64,128]{3,2,1,0:T(8,128)S(1)} %get-tuple-element.33.refs_0_.refs_4_.fourth.refs_6_), channel_id=1, source_target_pairs={{0,8},{8,0},{16,24},{24,16},{1,9},{9,1},{17,25},{25,17},{2,10},{10... | collective-permute-start | bytes 786440 | tf_op jit(solution)/shard_map/ppermute | solution.py:523
  10.2 10.9 %collective-permute-start.9 = (f32[2,4,64,128]{3,2,1,0:T(8,128)S(1)}, f32[2,4,64,128]{3,2,1,0:T(8,128)S(1)}, u32[]{:S(2)}, u32[]{:S(2)}) collective-permute-start(f32[2,4,64,128]{3,2,1,0:T(8,128)S(1)} %collective-permute-done.8.refs_4_.refs_2_.refs_1_), channel_id=1, source_target_pairs={{0,16},{8,24},{16,0},{24,8},{1,17},{9,25},{17,1},{25,9},{2,18},{10... | collective-permute-start | bytes 786440 | tf_op jit(solution)/shard_map/ppermute | solution.py:528
  14.7 7.5 %collective-permute-start.7 = (f32[2,4,64,128]{3,2,1,0:T(8,128)S(1)}, f32[2,4,64,128]{3,2,1,0:T(8,128)S(1)}, u32[]{:S(2)}, u32[]{:S(2)}) collective-permute-start(f32[2,4,64,128]{3,2,1,0:T(8,128)S(1)} %collective-permute-done.6.refs_1_.refs_7_), channel_id=1, source_target_pairs={{0,16},{8,24},{16,0},{24,8},{1,17},{9,25},{17,1},{25,9},{2,18},{10... | collective-permute-start | bytes 786440 | tf_op jit(solution)/shard_map/ppermute | solution.py:528
  17.5 9.2 %collective-permute-start.17 = (f32[2,4,64,128]{3,2,1,0:T(8,128)S(1)}, f32[2,4,64,128]{3,2,1,0:T(8,128)S(1)}, u32[]{:S(2)}, u32[]{:S(2)}) collective-permute-start(f32[2,4,64,128]{3,2,1,0:T(8,128)S(1)} %get-tuple-element.41.second.refs_1_.refs_3_.refs_0_.refs_2_), channel_id=1, source_target_pairs={{0,8},{8,0},{16,24},{24,16},{1,9},{9,1},{17,25},{25,17},{2,10},{10... | collective-permute-start | bytes 786440 | tf_op jit(solution)/shard_map/ppermute | solution.py:523
  19.1 13.3 %collective-permute-start.15 = (f32[2,4,64,128]{3,2,1,0:T(8,128)S(1)}, f32[2,4,64,128]{3,2,1,0:T(8,128)S(1)}, u32[]{:S(2)}, u32[]{:S(2)}) collective-permute-start(f32[2,4,64,128]{3,2,1,0:T(8,128)S(1)} %get-tuple-element.44.refs_2_.refs_0_.refs_4_), channel_id=1, source_target_pairs={{0,8},{8,0},{16,24},{24,16},{1,9},{9,1},{17,25},{25,17},{2,10},{10... | collective-permute-start | bytes 786440 | tf_op jit(solution)/shard_map/ppermute | solution.py:523
  19.6 18.4 %collective-permute-start.13 = (f32[2,4,64,128]{3,2,1,0:T(8,128)S(1)}, f32[2,4,64,128]{3,2,1,0:T(8,128)S(1)}, u32[]{:S(2)}, u32[]{:S(2)}) collective-permute-start(f32[2,4,64,128]{3,2,1,0:T(8,128)S(1)} %get-tuple-element.37.refs_0_.refs_3_.refs_2_.refs_4_), channel_id=1, source_target_pairs={{0,8},{8,0},{16,24},{24,16},{1,9},{9,1},{17,25},{25,17},{2,10},{10... | collective-permute-start | bytes 786440 | tf_op jit(solution)/shard_map/ppermute | solution.py:523
  22.3 42.0 %collective-permute-start.10 = (f32[6,4,64,128]{3,2,1,0:T(8,128)S(1)}, f32[6,4,64,128]{3,2,1,0:T(8,128)S(1)}, u32[]{:S(2)}, u32[]{:S(2)}) collective-permute-start(f32[6,4,64,128]{3,2,1,0:T(8,128)S(1)} %get-tuple-element.34), channel_id=1, source_target_pairs={{0,1},{1,0},{2,3},{3,2},{4,5},{5,4},{6,7},{7,6},{8,9},{9,8},{10,11... | collective-permute-start | bytes 2359304 | tf_op jit(solution)/shard_map/ppermute | solution.py:427
  22.4 53.9 %collective-permute-start.11 = (f32[6,4,64,128]{3,2,1,0:T(8,128)S(1)}, f32[6,4,64,128]{3,2,1,0:T(8,128)S(1)}, u32[]{:S(2)}, u32[]{:S(2)}) collective-permute-start(f32[6,4,64,128]{3,2,1,0:T(8,128)S(1)} %get-tuple-element.35), channel_id=1, source_target_pairs={{1,2},{3,4},{5,6},{2,1},{4,3},{6,5},{9,10},{11,12},{13,14},{10,9},... | collective-permute-start | bytes 2359304 | tf_op jit(solution)/shard_map/ppermute | solution.py:426
  26.8 16.9 %collective-permute-start = (f32[2,4,64,128]{3,2,1,0:T(8,128)S(1)}, f32[2,4,64,128]{3,2,1,0:T(8,128)S(1)}, u32[]{:S(2)}, u32[]{:S(2)}) collective-permute-start(f32[2,4,64,128]{3,2,1,0:T(8,128)S(1)} %get-tuple-element.30.refs_1_.refs_0_.refs_2_.refs_4_), channel_id=1, source_target_pairs={{0,8},{8,0},{16,24},{24,16},{1,9},{9,1},{17,25},{25,17},{2,10},{10... | collective-permute-start | bytes 786440 | tf_op jit(solution)/shard_map/ppermute | solution.py:523
  32.4 14.6 %collective-permute-start.2 = (f32[2,4,64,128]{3,2,1,0:T(8,128)S(1)}, f32[2,4,64,128]{3,2,1,0:T(8,128)S(1)}, u32[]{:S(2)}, u32[]{:S(2)}) collective-permute-start(f32[2,4,64,128]{3,2,1,0:T(8,128)S(1)} %get-tuple-element.31.refs_2_.refs_4_), channel_id=1, source_target_pairs={{0,8},{8,0},{16,24},{24,16},{1,9},{9,1},{17,25},{25,17},{2,10},{10... | collective-permute-start | bytes 786440 | tf_op jit(solution)/shard_map/ppermute | solution.py:523
  38.0 9.5 %collective-permute-start.4 = (f32[2,4,64,128]{3,2,1,0:T(8,128)S(1)}, f32[2,4,64,128]{3,2,1,0:T(8,128)S(1)}, u32[]{:S(2)}, u32[]{:S(2)}) collective-permute-start(f32[2,4,64,128]{3,2,1,0:T(8,128)S(1)} %get-tuple-element.32.refs_3_.third.refs_4_), channel_id=1, source_target_pairs={{0,16},{8,24},{16,0},{24,8},{1,17},{9,25},{17,1},{25,9},{2,18},{10... | collective-permute-start | bytes 786440 | tf_op jit(solution)/shard_map/ppermute | solution.py:533
  43.6 9.0 %collective-permute-start.18 = (f32[2,4,64,128]{3,2,1,0:T(8,128)S(1)}, f32[2,4,64,128]{3,2,1,0:T(8,128)S(1)}, u32[]{:S(2)}, u32[]{:S(2)}) collective-permute-start(f32[2,4,64,128]{3,2,1,0:T(8,128)S(1)} %collective-permute-done.17.refs_4_.refs_1_.refs_3_), channel_id=1, source_target_pairs={{0,16},{8,24},{16,0},{24,8},{1,17},{9,25},{17,1},{25,9},{2,18},{10... | collective-permute-start | bytes 786440 | tf_op jit(solution)/shard_map/ppermute | solution.py:528
  47.0 11.2 %collective-permute-start.16 = (f32[2,4,64,128]{3,2,1,0:T(8,128)S(1)}, f32[2,4,64,128]{3,2,1,0:T(8,128)S(1)}, u32[]{:S(2)}, u32[]{:S(2)}) collective-permute-start(f32[2,4,64,128]{3,2,1,0:T(8,128)S(1)} %collective-permute-done.15.refs_1_.refs_3_.refs_5_), channel_id=1, source_target_pairs={{0,16},{8,24},{16,0},{24,8},{1,17},{9,25},{17,1},{25,9},{2,18},{10... | collective-permute-start | bytes 786440 | tf_op jit(solution)/shard_map/ppermute | solution.py:528
  47.5 16.3 %collective-permute-start.14 = (f32[2,4,64,128]{3,2,1,0:T(8,128)S(1)}, f32[2,4,64,128]{3,2,1,0:T(8,128)S(1)}, u32[]{:S(2)}, u32[]{:S(2)}) collective-permute-start(f32[2,4,64,128]{3,2,1,0:T(8,128)S(1)} %collective-permute-done.13.refs_1_.refs_3_.refs_5_), channel_id=1, source_target_pairs={{0,16},{8,24},{16,0},{24,8},{1,17},{9,25},{17,1},{25,9},{2,18},{10... | collective-permute-start | bytes 786440 | tf_op jit(solution)/shard_map/ppermute | solution.py:528
  52.6 26.5 %collective-permute-start.12 = (f32[2,4,64,128]{3,2,1,0:T(8,128)S(1)}, f32[2,4,64,128]{3,2,1,0:T(8,128)S(1)}, u32[]{:S(2)}, u32[]{:S(2)}) collective-permute-start(f32[2,4,64,128]{3,2,1,0:T(8,128)S(1)} %get-tuple-element.32.refs_3_.third.refs_4_), channel_id=1, source_target_pairs={{0,8},{8,0},{16,24},{24,16},{1,9},{9,1},{17,25},{25,17},{2,10},{10... | collective-permute-start | bytes 786440 | tf_op jit(solution)/shard_map/ppermute | solution.py:523
  58.2 24.7 %collective-permute-start.1 = (f32[2,4,64,128]{3,2,1,0:T(8,128)S(1)}, f32[2,4,64,128]{3,2,1,0:T(8,128)S(1)}, u32[]{:S(2)}, u32[]{:S(2)}) collective-permute-start(f32[2,4,64,128]{3,2,1,0:T(8,128)S(1)} %collective-permute-done.refs_1_.refs_3_.refs_5_), channel_id=1, source_target_pairs={{0,16},{8,24},{16,0},{24,8},{1,17},{9,25},{17,1},{25,9},{2,18},{10... | collective-permute-start | bytes 786440 | tf_op jit(solution)/shard_map/ppermute | solution.py:528
  63.8 20.3 %collective-permute-start.3 = (f32[2,4,64,128]{3,2,1,0:T(8,128)S(1)}, f32[2,4,64,128]{3,2,1,0:T(8,128)S(1)}, u32[]{:S(2)}, u32[]{:S(2)}) collective-permute-start(f32[2,4,64,128]{3,2,1,0:T(8,128)S(1)} %collective-permute-done.2.refs_3_.refs_5_), channel_id=1, source_target_pairs={{0,16},{8,24},{16,0},{24,8},{1,17},{9,25},{17,1},{25,9},{2,18},{10... | collective-permute-start | bytes 786440 | tf_op jit(solution)/shard_map/ppermute | solution.py:528
  64.3 21.0 %collective-permute-start.5 = (f32[2,4,64,128]{3,2,1,0:T(8,128)S(1)}, f32[2,4,64,128]{3,2,1,0:T(8,128)S(1)}, u32[]{:S(2)}, u32[]{:S(2)}) collective-permute-start(f32[2,4,64,128]{3,2,1,0:T(8,128)S(1)} %collective-permute-done.4), channel_id=1, source_target_pairs={{0,8},{8,0},{16,24},{24,16},{1,9},{9,1},{17,25},{25,17},{2,10},{10... | collective-permute-start | bytes 786440 | tf_op jit(solution)/shard_map/ppermute | solution.py:523
